TPU v7x, 512 devices: a whole 4x8x8 slice. The times are simulated.
512 devices in a mesh: seq: 64 (over z, y_lo, core), head: 8 (over y_hi, x).
Axes of the slice: x: 4, y: 8 (y_hi: 2, y_lo: 4; y = y_hi * 4 + y_lo), z: 8, core: 2. Of those that a mesh axis runs over, the one named last changes fastest.
Arguments:
- query: bfloat16 [32768, 32, 128], P('seq', 'head'), may hold values from -6 to 6
- key: bfloat16 [32768, 16, 128], P('seq', 'head'), may hold values from -6 to 6
- value: bfloat16 [32768, 16, 128], P('seq', 'head'), may hold values from -6 to 6
- grad_out: bfloat16 [32768, 32, 128], P('seq', 'head'), may hold values from -25 to 25
- q_gain: float32 [128], replicated, may hold values from 0.1 to 1.9
- k_gain: float32 [128], replicated, may hold values from 0.1 to 1.9
Outputs:
- grad_query: bfloat16 [32768, 32, 128], P('seq', 'head')
- grad_key: bfloat16 [32768, 16, 128], P('seq', 'head')
- grad_value: bfloat16 [32768, 16, 128], P('seq', 'head')
- grad_q_gain: float32 [128], replicated
- grad_k_gain: float32 [128], replicated
All inputs are finite; a program needn't handle non-finite values.
Results may differ from a plain program's by a relative error of at most 0.0099.
Values may be sent and summed in bfloat16 or wider, within the bound.
A program may use at most 64 MiB of HBM per device.

v0:
```python
import jax
import jax.numpy as jnp
from jax import lax
from jax.sharding import PartitionSpec as P

WINDOW = 1024


score_scale = 168.0 ** (-0.5)
norm_eps = 1e-06


def passed_along(value, axis, steps):
    count = lax.axis_size(axis)
    initial, last = (max(0, -steps), min(count, count - steps))
    return lax.ppermute(value, axis, [(source, source + steps) for source in range(initial, last)])


def normalize(inputs_raw, gain_vec):
    as_float = inputs_raw.astype(jnp.float32)
    inverse_rms = lax.rsqrt(jnp.mean(as_float * as_float, axis=-1, keepdims=True) + norm_eps)
    unit_rows = as_float * inverse_rms
    return (unit_rows * gain_vec, unit_rows, inverse_rms)


def norm_back(d_normed, unit_rows, inverse_rms, gain_vec):
    d_unit = d_normed * gain_vec
    d_inputs = inverse_rms * (
        d_unit - unit_rows * jnp.mean(d_unit * unit_rows, axis=-1, keepdims=True)
    )
    d_gain = jnp.sum(d_normed * unit_rows, axis=(0, 1))
    return (d_inputs, d_gain)


def head_grads(query_head, key_head, value_head, incoming_gradient, allowed):
    last_last = (((1,), (1,)), ((), ()))
    first_first = (((0,), (0,)), ((), ()))
    scores = score_scale * lax.dot_general(
        query_head, key_head, last_last, preferred_element_type=jnp.float32
    )
    exp_scores = jnp.where(allowed, jnp.exp(scores), 0.0)
    attn_probs = exp_scores / jnp.sum(exp_scores, axis=1, keepdims=True)
    probs_low = attn_probs.astype(jnp.bfloat16)
    attended = jnp.dot(probs_low, value_head, preferred_element_type=jnp.float32)
    offset = jnp.sum(incoming_gradient.astype(jnp.float32) * attended, axis=1, keepdims=True)
    d_probs = lax.dot_general(
        incoming_gradient, value_head, last_last, preferred_element_type=jnp.float32
    )
    d_scores = (attn_probs * (d_probs - offset)).astype(jnp.bfloat16)
    value_grad = lax.dot_general(
        probs_low, incoming_gradient, first_first, preferred_element_type=jnp.float32
    )
    query_grad = score_scale * jnp.dot(d_scores, key_head, preferred_element_type=jnp.float32)
    key_grad = score_scale * lax.dot_general(
        d_scores, query_head, first_first, preferred_element_type=jnp.float32
    )
    return (query_grad, key_grad, value_grad)


def per_device(query, key, value, grad_out, q_gain, k_gain):
    rows_dev, heads_dev, head_width = query.shape
    kv_dev = key.shape[1]
    heads_per_group = heads_dev // kv_dev
    reach_total = (WINDOW + rows_dev - 1) // rows_dev
    key_span = (reach_total + 1) * rows_dev
    shard_index = lax.axis_index("seq")
    q_normed, q_unit, q_inverse = normalize(query, q_gain)
    k_normed, k_unit, k_inverse = normalize(key, k_gain)
    query_low = q_normed.astype(jnp.bfloat16)
    key_low = k_normed.astype(jnp.bfloat16)
    earlier = [
        passed_along((key_low, value), "seq", distance) for distance in range(1, reach_total + 1)
    ]
    keys_all = jnp.concatenate([received[0] for received in earlier[::-1]] + [key_low], axis=0)
    values_all = jnp.concatenate([received[1] for received in earlier[::-1]] + [value], axis=0)
    row_ids = jnp.arange(rows_dev, dtype=jnp.int32)[:, None]
    col_ids = jnp.arange(key_span, dtype=jnp.int32)[None, :]
    distance_grid = row_ids + reach_total * rows_dev - col_ids
    allowed = (
        (distance_grid >= 0)
        & (distance_grid < WINDOW)
        & (col_ids + shard_index * rows_dev >= reach_total * rows_dev)
    )
    query_heads = jnp.transpose(query_low, (1, 0, 2))
    upstream_heads = jnp.transpose(grad_out, (1, 0, 2))

    def per_head(unused, inputs):
        head_id, query_head, incoming_gradient = inputs
        kv_index = head_id // heads_per_group
        key_head = lax.dynamic_index_in_dim(keys_all, kv_index, 1, keepdims=False)
        value_head = lax.dynamic_index_in_dim(values_all, kv_index, 1, keepdims=False)
        return (unused, head_grads(query_head, key_head, value_head, incoming_gradient, allowed))

    head_ids = jnp.arange(heads_dev, dtype=jnp.int32)
    unused, (query_parts, key_parts, value_parts) = lax.scan(
        per_head, 0, (head_ids, query_heads, upstream_heads)
    )
    query_grad_n = jnp.transpose(query_parts, (1, 0, 2))
    key_sum = jnp.transpose(
        key_parts.reshape(kv_dev, heads_per_group, key_span, head_width).sum(axis=1), (1, 0, 2)
    )
    value_sum = jnp.transpose(
        value_parts.reshape(kv_dev, heads_per_group, key_span, head_width).sum(axis=1), (1, 0, 2)
    )
    own_start = reach_total * rows_dev
    key_total = key_sum[own_start:]
    value_total = value_sum[own_start:]
    for distance in range(1, reach_total + 1):
        low_row = (reach_total - distance) * rows_dev
        back_key, back_value = passed_along(
            (key_sum[low_row : low_row + rows_dev], value_sum[low_row : low_row + rows_dev]),
            "seq",
            -distance,
        )
        key_total = key_total + back_key
        value_total = value_total + back_value
    grad_query, q_gain_part = norm_back(query_grad_n, q_unit, q_inverse, q_gain)
    grad_key, k_gain_part = norm_back(key_total, k_unit, k_inverse, k_gain)
    grad_q_gain, grad_k_gain = lax.psum((q_gain_part, k_gain_part), ("seq", "head"))
    return (
        grad_query.astype(jnp.bfloat16),
        grad_key.astype(jnp.bfloat16),
        value_total.astype(jnp.bfloat16),
        grad_q_gain,
        grad_k_gain,
    )


def solution(mesh):
    return jax.shard_map(
        per_device,
        mesh=mesh,
        in_specs=(
            P("seq", "head", None),
            P("seq", "head", None),
            P("seq", "head", None),
            P("seq", "head", None),
            P(),
            P(),
        ),
        out_specs=(
            P("seq", "head", None),
            P("seq", "head", None),
            P("seq", "head", None),
            P(),
            P(),
        ),
        check_vma=False,
    )
```

profile of v0, /device:TPU:1, one launch (start us, length us, event | category | flops | bytes accessed | tf_op | source)
XLA Modules:
  0.0 241.3 jit_solution(13102099941542296514)
XLA Ops:
  0.6 1.2 fusion.59
  1.8 1.2 fusion.53
  3.0 4.0 %collective-permute-start = (bf16[512,2,128]{2,0,1:T(8,128)(2,1)S(1)}, bf16[512,2,128]{2,0,1:T(8,128)(2,1)S(1)}, u32[]{:S(2)}, u32[]{:S(2)}) collective-permute-start(bf16[512,2,128]{2,0,1:T(8,128)(2,1)S(1)} %fusion.53), channel_id=1, source_target_pairs={{0,16},{8,24},{16,32},{24,40},{32,48},{40,56},{48,64},{56,72},{64,... | collective-permute-start | bytes 786440 | tf_op jit(solution)/shard_map/ppermute | solution.py:16
  7.0 4.0 %collective-permute-start.1 = (bf16[512,2,128]{2,0,1:T(8,128)(2,1)S(1)}, bf16[512,2,128]{2,0,1:T(8,128)(2,1)}, u32[]{:S(2)}, u32[]{:S(2)}) collective-permute-start(bf16[512,2,128]{2,0,1:T(8,128)(2,1)S(1)} %fusion.53), channel_id=1, source_target_pairs={{0,8},{8,16},{16,24},{24,32},{32,40},{40,48},{48,56},{56,64},{64,7... | collective-permute-start | bytes 786440 | tf_op jit(solution)/shard_map/ppermute | solution.py:16
  11.1 1.0 copy.23
  12.1 3.2 %collective-permute-start.2 = (bf16[512,2,128]{2,0,1:T(8,128)(2,1)S(1)}, bf16[512,2,128]{2,0,1:T(8,128)(2,1)S(1)}, u32[]{:S(2)}, u32[]{:S(2)}) collective-permute-start(bf16[512,2,128]{2,0,1:T(8,128)(2,1)S(1)} %copy.23), channel_id=1, source_target_pairs={{0,16},{8,24},{16,32},{24,40},{32,48},{40,56},{48,64},{56,72},{64,... | collective-permute-start | bytes 786440 | tf_op jit(solution)/shard_map/ppermute | solution.py:16
  15.3 2.2 collective-permute-start.3
  17.5 1.7 fusion.48
  19.2 1.7 fusion.60
  21.0 2.1 copy.22
  23.2 0.7 copy-done.4
  23.9 1.1 pad_maximum_fusion
  25.0 0.7 collective-permute-done.3
  25.6 1.9 pad_maximum_fusion.1
  27.5 64.0 %while.17 = (s32[]{:T(128)}, f32[4,512,128]{2,0,1:T(4,128)S(1)}, f32[4,1536,128]{2,1,0:T(8,128)}, f32[4,1536,128]{2,1,0:T(8,128)}, bf16[4,512,128]{2,1,0:T(8,128...) while((s32[]{:T(128)}, f32[4,512,128]{2,0,1:T(4,128)S(1)}, ...), condition=%wide.region_5.6_spmd.clone, body=%wide.region_2.5_spmd.clone.sunk | while | flops 1221000192 | bytes 27150760 | solution.py:95
  27.5 0.6 dynamic_slice.94
  30.7 1.6 fusion.95
  32.3 1.6 fusion.99
  34.0 0.8 fusion.96
  34.7 0.8 fusion.97
  35.6 1.5 fusion.98
  37.1 0.6 convolution_multiply_fusion.5
  37.6 5.8 %dynamic_update_slice.30 = f32[4,512,128]{2,0,1:T(4,128)S(1)} dynamic-update-slice(f32[4,512,128]{2,0,1:T(4,128)S(1)} %get-tuple-element.322, f32[1,512,128]{2,0,1:T(1,128)S(1)} %bitcast.85, s32[]{:T(128)} %get-tuple-element.321, s32[]{:T(128)} %constant.86.clone.1..sunk, s32[]{:T(128)} %constant.86.clone.1..sunk) | dynamic-update-slice | bytes 524292 | tf_op jit(solution)/shard_map/while/body/jit(dynamic_update_index_in_dim)/dynamic_update_slice | solution.py:95
  43.5 0.6 dynamic_slice.94
  46.7 1.6 fusion.95
  48.3 1.6 fusion.99
  49.9 0.8 fusion.96
  50.7 0.8 fusion.97
  51.5 1.5 fusion.98
  53.1 0.6 convolution_multiply_fusion.5
  53.6 5.8 %dynamic_update_slice.30 = f32[4,512,128]{2,0,1:T(4,128)S(1)} dynamic-update-slice(f32[4,512,128]{2,0,1:T(4,128)S(1)} %get-tuple-element.322, f32[1,512,128]{2,0,1:T(1,128)S(1)} %bitcast.85, s32[]{:T(128)} %get-tuple-element.321, s32[]{:T(128)} %constant.86.clone.1..sunk, s32[]{:T(128)} %constant.86.clone.1..sunk) | dynamic-update-slice | bytes 524292 | tf_op jit(solution)/shard_map/while/body/jit(dynamic_update_index_in_dim)/dynamic_update_slice | solution.py:95
  59.4 0.6 dynamic_slice.94
  62.7 1.6 fusion.95
  64.3 1.7 fusion.99
  65.9 0.8 fusion.96
  66.7 0.8 fusion.97
  67.5 1.5 fusion.98
  69.0 0.6 convolution_multiply_fusion.5
  69.6 5.8 %dynamic_update_slice.30 = f32[4,512,128]{2,0,1:T(4,128)S(1)} dynamic-update-slice(f32[4,512,128]{2,0,1:T(4,128)S(1)} %get-tuple-element.322, f32[1,512,128]{2,0,1:T(1,128)S(1)} %bitcast.85, s32[]{:T(128)} %get-tuple-element.321, s32[]{:T(128)} %constant.86.clone.1..sunk, s32[]{:T(128)} %constant.86.clone.1..sunk) | dynamic-update-slice | bytes 524292 | tf_op jit(solution)/shard_map/while/body/jit(dynamic_update_index_in_dim)/dynamic_update_slice | solution.py:95
  75.4 0.6 dynamic_slice.94
  78.6 1.6 fusion.95
  80.2 1.7 fusion.99
  81.9 0.8 fusion.96
  82.7 0.8 fusion.97
  83.6 1.5 fusion.98
  85.1 0.6 convolution_multiply_fusion.5
  85.7 5.8 %dynamic_update_slice.30 = f32[4,512,128]{2,0,1:T(4,128)S(1)} dynamic-update-slice(f32[4,512,128]{2,0,1:T(4,128)S(1)} %get-tuple-element.322, f32[1,512,128]{2,0,1:T(1,128)S(1)} %bitcast.85, s32[]{:T(128)} %get-tuple-element.321, s32[]{:T(128)} %constant.86.clone.1..sunk, s32[]{:T(128)} %constant.86.clone.1..sunk) | dynamic-update-slice | bytes 524292 | tf_op jit(solution)/shard_map/while/body/jit(dynamic_update_index_in_dim)/dynamic_update_slice | solution.py:95
  91.5 2.4 bitcast_reduce_fusion.1
  94.0 2.2 collective-permute-start.4
  96.2 1.3 collective-permute-start.5
  97.5 1.6 fusion.47
  99.1 2.3 bitcast_reduce_fusion
  101.5 1.9 collective-permute-start.6
  103.4 1.3 collective-permute-start.7
  104.7 2.5 %fusion.46 = bf16[512,4,128]{2,1,0:T(4,128)(2,1)} fusion(bf16[512,4,128]{2,1,0:T(4,128)(2,1)S(1)} %copy-done, f32[4,512,128]{2,0,1:T(4,128)S(1)} %get-tuple-element.133, f32[512,4]{1,0:T(8,128)S(1)} %broadcast_multiply_fusion, f32[128]{0:T(128)S(1)} %copy-done.6, f32[512,4]{1,0:T(8,128)S(1)} %add_rsqrt_fusion), kind=kLoop, calls=%fused_computation.57 | loop fusion | flops 1835008 | bytes 2114048 | tf_op jit(solution)/shard_map/convert_element_type | solution.py:121
  107.3 1.9 collective-permute-done.4
  109.2 3.8 %collective-permute-done.5 = f32[512,2,128]{2,0,1:T(8,128)S(1)} collective-permute-done((f32[512,2,128]{2,0,1:T(8,128)S(1)}, f32[512,2,128]{2,0,1:T(8,128)S(1)}, u32[]{:S(2)}, u32[]{:S(2)}) %collective-permute-start.5) | collective-permute-done | bytes 524320 | tf_op jit(solution)/shard_map/ppermute | solution.py:16
  113.0 0.4 fusion.58
  113.4 0.3 fusion.57
  113.7 1.0 copy.28
  114.7 13.1 %collective-permute-done.6 = f32[512,2,128]{2,0,1:T(8,128)S(1)} collective-permute-done((f32[512,2,128]{2,0,1:T(8,128)S(1)}, f32[512,2,128]{2,0,1:T(8,128)S(1)}, u32[]{:S(2)}, u32[]{:S(2)}) %collective-permute-start.6) | collective-permute-done | bytes 524320 | tf_op jit(solution)/shard_map/ppermute | solution.py:16
  127.8 0.1 fusion.62
  127.9 1.0 copy.29
  128.9 112.4 %all-reduce = (f32[128]{0:T(128)}, f32[128]{0:T(128)}) all-reduce(f32[128]{0:T(128)S(1)} %get-tuple-element.200, f32[128]{0:T(128)S(1)} %get-tuple-element.202), channel_id=1, replica_groups=mesh['seq'=64,'head'=8] {'seq','head'}, use_global_device_ids=true, to_apply=%region_11.12 | all-reduce | flops 256 | bytes 2048 | tf_op jit(solution)/shard_map/psum | solution.py:119
  (42 shorter events, 0.4 us)
Async XLA Ops:
  3.0 20.2 %collective-permute-start = (bf16[512,2,128]{2,0,1:T(8,128)(2,1)S(1)}, bf16[512,2,128]{2,0,1:T(8,128)(2,1)S(1)}, u32[]{:S(2)}, u32[]{:S(2)}) collective-permute-start(bf16[512,2,128]{2,0,1:T(8,128)(2,1)S(1)} %fusion.53), channel_id=1, source_target_pairs={{0,16},{8,24},{16,32},{24,40},{32,48},{40,56},{48,64},{56,72},{64,... | collective-permute-start | bytes 786440 | tf_op jit(solution)/shard_map/ppermute | solution.py:16
  7.0 16.8 %collective-permute-start.1 = (bf16[512,2,128]{2,0,1:T(8,128)(2,1)S(1)}, bf16[512,2,128]{2,0,1:T(8,128)(2,1)}, u32[]{:S(2)}, u32[]{:S(2)}) collective-permute-start(bf16[512,2,128]{2,0,1:T(8,128)(2,1)S(1)} %fusion.53), channel_id=1, source_target_pairs={{0,8},{8,16},{16,24},{24,32},{32,40},{40,48},{48,56},{56,64},{64,7... | collective-permute-start | bytes 786440 | tf_op jit(solution)/shard_map/ppermute | solution.py:16
  12.1 12.9 %collective-permute-start.2 = (bf16[512,2,128]{2,0,1:T(8,128)(2,1)S(1)}, bf16[512,2,128]{2,0,1:T(8,128)(2,1)S(1)}, u32[]{:S(2)}, u32[]{:S(2)}) collective-permute-start(bf16[512,2,128]{2,0,1:T(8,128)(2,1)S(1)} %copy.23), channel_id=1, source_target_pairs={{0,16},{8,24},{16,32},{24,40},{32,48},{40,56},{48,64},{56,72},{64,... | collective-permute-start | bytes 786440 | tf_op jit(solution)/shard_map/ppermute | solution.py:16
  15.3 10.3 %collective-permute-start.3 = (bf16[512,2,128]{2,0,1:T(8,128)(2,1)S(1)}, bf16[512,2,128]{2,0,1:T(8,128)(2,1)}, u32[]{:S(2)}, u32[]{:S(2)}) collective-permute-start(bf16[512,2,128]{2,0,1:T(8,128)(2,1)S(1)} %copy.23), channel_id=1, source_target_pairs={{0,8},{8,16},{16,24},{24,32},{32,40},{40,48},{48,56},{56,64},{64,7... | collective-permute-start | bytes 786440 | tf_op jit(solution)/shard_map/ppermute | solution.py:16
  23.1 0.7 copy-start.4
  30.7 1.6 copy-start.3
  32.3 1.7 copy-start.2
  46.7 1.6 copy-start.3
  48.3 1.7 copy-start.2
  62.6 1.6 copy-start.3
  64.2 1.7 copy-start.2
  78.6 1.6 copy-start.3
  80.2 1.7 copy-start.2
  91.5 6.0 %copy-start = (bf16[512,4,128]{2,1,0:T(4,128)(2,1)S(1)}, bf16[512,4,128]{2,1,0:T(4,128)(2,1)}, u32[]{:S(2)}) copy-start(bf16[512,4,128]{2,1,0:T(4,128)(2,1)} %param.8) | copy-start | bytes 1572868
  91.5 6.0 %copy-start.6 = (f32[128]{0:T(128)S(1)}, f32[128]{0:T(128)}, u32[]{:S(2)}) copy-start(f32[128]{0:T(128)} %param.12) | copy-start | bytes 1540
  94.0 15.2 %collective-permute-start.4 = (f32[512,2,128]{2,0,1:T(8,128)S(1)}, f32[512,2,128]{2,0,1:T(8,128)S(1)}, u32[]{:S(2)}, u32[]{:S(2)}) collective-permute-start(f32[512,2,128]{2,0,1:T(8,128)S(1)} %get-tuple-element.233), channel_id=1, source_target_pairs={{8,0},{16,8},{24,16},{32,24},{40,32},{48,40},{56,48},{64,56},{72,6... | collective-permute-start | bytes 1572872 | tf_op jit(solution)/shard_map/ppermute | solution.py:16
  96.2 16.8 %collective-permute-start.5 = (f32[512,2,128]{2,0,1:T(8,128)S(1)}, f32[512,2,128]{2,0,1:T(8,128)S(1)}, u32[]{:S(2)}, u32[]{:S(2)}) collective-permute-start(f32[512,2,128]{2,0,1:T(8,128)S(1)} %get-tuple-element.234), channel_id=1, source_target_pairs={{16,0},{24,8},{32,16},{40,24},{48,32},{56,40},{64,48},{72,56},{80,... | collective-permute-start | bytes 1572872 | tf_op jit(solution)/shard_map/ppermute | solution.py:16
  101.4 11.6 %copy-start.1 = (bf16[512,2,128]{2,1,0:T(2,128)(2,1)S(1)}, bf16[512,2,128]{2,1,0:T(2,128)(2,1)}, u32[]{:S(2)}) copy-start(bf16[512,2,128]{2,1,0:T(2,128)(2,1)} %param.9) | copy-start | bytes 786436
  101.4 11.6 %copy-start.5 = (f32[128]{0:T(128)S(1)}, f32[128]{0:T(128)}, u32[]{:S(2)}) copy-start(f32[128]{0:T(128)} %param.13) | copy-start | bytes 1540
  101.5 26.3 %collective-permute-start.6 = (f32[512,2,128]{2,0,1:T(8,128)S(1)}, f32[512,2,128]{2,0,1:T(8,128)S(1)}, u32[]{:S(2)}, u32[]{:S(2)}) collective-permute-start(f32[512,2,128]{2,0,1:T(8,128)S(1)} %get-tuple-element.231), channel_id=1, source_target_pairs={{8,0},{16,8},{24,16},{32,24},{40,32},{48,40},{56,48},{64,56},{72,6... | collective-permute-start | bytes 1572872 | tf_op jit(solution)/shard_map/ppermute | solution.py:16
  103.4 24.4 %collective-permute-start.7 = (f32[512,2,128]{2,0,1:T(8,128)S(1)}, f32[512,2,128]{2,0,1:T(8,128)S(1)}, u32[]{:S(2)}, u32[]{:S(2)}) collective-permute-start(f32[512,2,128]{2,0,1:T(8,128)S(1)} %get-tuple-element.232), channel_id=1, source_target_pairs={{16,0},{24,8},{32,16},{40,24},{48,32},{56,40},{64,48},{72,56},{80,... | collective-permute-start | bytes 1572872 | tf_op jit(solution)/shard_map/ppermute | solution.py:16
where the time goes:
time: 242 us; the launch traced here: 241 us
  blocking collectives  112 us (46%)
  local copies, waits for them, and re-layouts  31.5 us (13%)
  matrix products  27.7 us (11%)
  starting transfers between devices  20.2 us (8%)
  waiting for transfers between devices  19.5 us (8%)
  other arithmetic  18.4 us (8%)
  loops' own time  10.7 us (4%)
    psum x1, blocking collectives, per_device(): lax.psum((q_gain_part, k_gain_part), ('seq', 'head'))  112 us
    dynamic_update_slice x4, local copies, waits for them, and re-layouts, per_device(): lax.scan(per_head, 0, (head_ids, query_heads, upstream_heads))  23.2 us
    ppermute x8, starting transfers between devices, passed_along(): lax.ppermute(value, axis, [(source, source + steps) for source in range(i...  20.2 us
    ppermute x8, waiting for transfers between devices, passed_along(): lax.ppermute(value, axis, [(source, source + steps) for source in range(i...  19.5 us
    another operation x1, loops' own time, per_device(): lax.scan(per_head, 0, (head_ids, query_heads, upstream_heads))  10.7 us
    dot_general x4, matrix products, head_grads(): lax.dot_general(probs_low, incoming_gradient, first_first, preferred_elem...  6.65 us
    dot_general x4, matrix products, head_grads(): lax.dot_general(query_head, key_head, last_last, preferred_element_type=j...  6.33 us
    dot_general x4, matrix products, head_grads(): lax.dot_general(d_scores, query_head, first_first, preferred_element_type...  6.05 us
  transfers between devices with their start and end apart: 8, of which 4 were waited for; matrix products, arithmetic and copies ran while one was open for 7% of the time, Pallas kernels for 0%

commit v1 on v0

v1 whole, which is shorter than its diff:
```python
import functools
import math

import jax
import jax.numpy as jnp
from jax import lax
from jax.experimental import pallas as pl
from jax.experimental.pallas import tpu as pltpu
from jax.sharding import PartitionSpec as P

WINDOW = 1024
SCALE = 168.0 ** (-0.5)
EXP2_SCALE = SCALE * math.log2(math.e)
EPS = 1e-06
CORES = 2
Y_LO = 4
Y_HI = 2

BF = jnp.bfloat16
F32 = jnp.float32
MESH = pl.DeviceIdType.MESH

T = 512
D = 128
B = 256
KEYS = 3 * T
EXT = 16


def dot_nn(a, b):
    return lax.dot_general(a, b, (((1,), (0,)), ((), ())), preferred_element_type=F32)


def dot_nt(a, b):
    return lax.dot_general(a, b, (((1,), (1,)), ((), ())), preferred_element_type=F32)


def transposed(x):
    return jnp.transpose(x.astype(F32)).astype(BF)


def kernel(
    sizes,
    q_in, k_in, v_in, g_in, q_gain, k_gain,
    gq_out, gk_out, gv_out, gain_out,
    q_buf, g_buf, k_buf, v_buf,
    q_unit, q_inv, k_unit, k_inv, stage,
    q_ext, q_low, g_t, g_ext,
    kv, v_ok, v_t, k_t, e_s, ds_s, av_s, dq_t,
    dk_s, dv_s, dq_s,
    send_b, recv_b, send_r, recv_r,
    red_src, red_y, red_z, red_x,
    in_sem, out_sem,
    f_send, f_recv, s_send, s_recv, b_send, b_recv, r_send, r_recv,
    ys_sem, yr_sem, zs_sem, zr_sem, xs_sem, xr_sem,
):
    n_seq, n_head = sizes
    n_z = n_seq // (CORES * Y_LO)
    n_x = n_head // Y_HI
    seq = lax.axis_index("seq")
    head = lax.axis_index("head")
    core = lax.rem(seq, CORES)
    y_lo = lax.rem(lax.div(seq, CORES), Y_LO)
    z = lax.div(seq, CORES * Y_LO)
    x = lax.rem(head, n_x)
    y_hi = lax.div(head, n_x)
    ahead = (lax.rem(seq + 2, n_seq), head)
    behind = (lax.rem(seq + n_seq - 2, n_seq), head)
    sibling = (seq + 1 - 2 * core, head)
    is_odd = core == 1
    is_even = core == 0

    n_y = Y_HI * Y_LO * CORES
    y_rank = (y_hi * Y_LO + y_lo) * CORES + core

    def y_peer(d):
        r = lax.rem(y_rank + d, n_y)
        c = lax.rem(r, CORES)
        yl = lax.rem(lax.div(r, CORES), Y_LO)
        yh = lax.div(r, CORES * Y_LO)
        return ((z * Y_LO + yl) * CORES + c, yh * n_x + x)

    def z_peer(d):
        return ((lax.rem(z + d, n_z) * Y_LO + y_lo) * CORES + core, head)

    def x_peer(d):
        return (seq, y_hi * n_x + lax.rem(x + d, n_x))

    peers = [ahead, behind, sibling]
    peers += [y_peer(d) for d in range(1, n_y)]
    peers += [z_peer(d) for d in range(1, n_z)]
    peers += [x_peer(d) for d in range(1, n_x)]

    ins = [
        pltpu.make_async_copy(src, dst, in_sem.at[i])
        for i, (src, dst) in enumerate(
            ((k_in, k_buf), (v_in, v_buf), (q_in, q_buf), (g_in, g_buf))
        )
    ]
    for c in ins:
        c.start()
    barrier = pltpu.get_barrier_semaphore()
    for p in peers:
        pl.semaphore_signal(barrier, inc=1, device_id=p, device_id_type=MESH)

    ok = [
        (seq >= 2).astype(F32),
        (seq >= 1).astype(F32),
        jnp.float32(1.0),
    ]

    def normalise(buf, unit, inv, rows):
        for r in range(0, rows, B):
            f = buf[r : r + B, :].astype(F32)
            i = lax.rsqrt(jnp.mean(f * f, axis=1, keepdims=True) + EPS)
            unit[r : r + B, :] = f * i
            inv[r : r + B, :] = jnp.broadcast_to(i, (B, D))

    kg = k_gain[...]
    qg = q_gain[...]
    ins[0].wait()
    normalise(k_buf, k_unit, k_inv, 2 * T)
    ins[1].wait()
    stage[: 2 * T, :] = v_buf[...].astype(F32)
    for kh in range(2):
        kv[2, kh, 0] = (k_unit[pl.ds(kh, T, stride=2), :] * kg).astype(BF)
        kv[2, kh, 1] = stage[pl.ds(kh, T, stride=2), :].astype(BF)
    pl.semaphore_wait(barrier, len(peers))

    def remote(src, dst, ssem, rsem, dev):
        return pltpu.make_async_remote_copy(
            src_ref=src, dst_ref=dst, send_sem=ssem, recv_sem=rsem, device_id=dev, device_id_type=MESH
        )

    fwd = [remote(kv.at[2, kh], kv.at[0, kh], f_send.at[kh], f_recv.at[kh], ahead) for kh in range(2)]
    sib_own = [remote(kv.at[2, kh], kv.at[1, kh], s_send.at[kh], s_recv.at[kh], sibling) for kh in range(2)]
    sib_fwd = [remote(kv.at[0, kh], kv.at[1, kh], s_send.at[kh], s_recv.at[kh], sibling) for kh in range(2)]
    ret_b = [remote(send_b.at[kh], recv_b.at[kh], b_send.at[kh], b_recv.at[kh], sibling) for kh in range(2)]
    ret_r = [remote(send_r.at[kh], recv_r.at[kh], r_send.at[kh], r_recv.at[kh], behind) for kh in range(2)]

    for kh in range(2):
        fwd[kh].start()

        @pl.when(is_even)
        def _(kh=kh):
            sib_own[kh].start()

    ins[2].wait()
    normalise(q_buf, q_unit, q_inv, 4 * T)
    ins[3].wait()
    stage[...] = g_buf[...].astype(F32)
    for kh in range(2):
        for qb in range(2):
            for h in range(2):
                rows = pl.ds(4 * B * qb + 2 * kh + h, B, stride=4)
                low = (q_unit[rows, :] * qg).astype(BF)
                scaled = low.astype(F32) * EXP2_SCALE
                high = scaled.astype(BF)
                rest = (scaled - high.astype(F32)).astype(BF)
                at = slice(h * B, (h + 1) * B)
                q_low[kh, qb, at, :] = low
                q_ext[kh, qb, at, :D] = high
                q_ext[kh, qb, at, D:] = rest
                g_t[kh, qb, :, at] = jnp.transpose(stage[rows, :]).astype(BF)

    def prepare(sh, kh):
        value = (kv[sh, kh, 1].astype(F32) * ok[sh]).astype(BF)
        span = slice(sh * T, (sh + 1) * T)
        v_ok[kh, span, :] = value
        v_t[kh, :D, span] = transposed(value)
        v_t[kh, D:, span] = jnp.full((EXT, T), ok[sh], F32).astype(BF)
        k_t[kh, :, span] = transposed(kv[sh, kh, 0])

    key_row = lax.broadcasted_iota(jnp.int32, (B, 2 * B), 0)
    query_col = lax.rem(lax.broadcasted_iota(jnp.int32, (B, 2 * B), 1), B)

    def pass1(kh, qb, r0, r1, first):
        off = qb * B
        for b in range(r0, r1, B):
            k = kv[b // T, kh, 0, b % T : b % T + B, :]
            s = dot_nt(jnp.concatenate([k, k], axis=1), q_ext[kh, qb])
            e = jnp.exp2(s)
            if b == off:
                e = jnp.where(key_row > query_col, e, 0.0)
            if b == off + WINDOW:
                e = jnp.where(key_row <= query_col, e, 0.0)
            e_s[kh, qb, b - off : b - off + B, :] = e.astype(BF)
        av = dot_nn(v_t[kh, :, r0:r1], e_s[kh, qb, r0 - off : r1 - off, :])
        if first:
            av_s[kh, qb] = av
        else:
            av_s[kh, qb] += av

    def finish(kh, qb):
        l_row = av_s[kh, qb, D : D + 1, :]
        inv = 1.0 / l_row
        scaled = (g_t[kh, qb].astype(F32) * inv).astype(BF)
        g_ext[kh, qb, :D, :] = scaled
        off = -inv * jnp.sum(scaled.astype(F32) * av_s[kh, qb, :D, :], axis=0, keepdims=True)
        high = off.astype(BF).astype(F32)
        rest = off - high
        row = lax.broadcasted_iota(jnp.int32, (EXT, 2 * B), 0)
        tail = jnp.where(row == 0, high, jnp.where(row == 1, rest, 0.0))
        g_ext[kh, qb, D : D + EXT, :] = tail.astype(BF)
        g_ext[kh, qb, D + EXT :, :] = jnp.zeros((D - EXT, 2 * B), BF)

    def pass2(kh, qb, r0, r1, first_q, first_of):
        off = qb * B
        for b in range(r0, r1, B):
            sh = b // T
            ones = jnp.full((B, D), ok[sh], F32).astype(BF)
            vx = jnp.concatenate([v_ok[kh, b : b + B, :], ones], axis=1)
            dp = dot_nn(vx, g_ext[kh, qb])
            e = e_s[kh, qb, b - off : b - off + B, :]
            ds = e * dp.astype(BF)
            ds_s[b - off : b - off + B, :] = ds
            dv = dot_nt(e, g_ext[kh, qb, :D, :])
            dk = dot_nn(ds, q_low[kh, qb])
            if first_of(b):
                dv_s[kh, b : b + B, :] = dv
                dk_s[kh, b : b + B, :] = dk
            else:
                dv_s[kh, b : b + B, :] += dv
                dk_s[kh, b : b + B, :] += dk
        dq = dot_nn(k_t[kh, :, r0:r1], ds_s[r0 - off : r1 - off, :])
        if first_q:
            dq_t[kh, qb] = dq
        else:
            dq_t[kh, qb] += dq

    for kh in range(2):
        prepare(2, kh)
        pass1(kh, 0, 2 * T, 2 * T + B, True)
        pass1(kh, 1, 2 * T, 3 * T, True)

    odd_f = is_odd.astype(F32)
    even_f = is_even.astype(F32)

    for kh in range(2):
        fwd[kh].wait_recv()

        @pl.when(is_odd)
        def _(kh=kh):
            sib_fwd[kh].start()

        prepare(0, kh)
        sib_own[kh].wait_recv()
        prepare(1, kh)
        pass1(kh, 0, 0, 2 * T, False)
        pass1(kh, 1, B, 2 * T, False)
        finish(kh, 0)
        finish(kh, 1)
        pass2(kh, 0, 0, 2 * T, True, lambda b: True)
        pass2(kh, 1, B, 2 * T, True, lambda b: False)
        send_b[kh, 0] = (dk_s[kh, T : 2 * T, :] * (SCALE * ok[1])).astype(BF)
        send_b[kh, 1] = (dv_s[kh, T : 2 * T, :] * ok[1]).astype(BF)
        ret_b[kh].start()
        pass2(kh, 0, 2 * T, 2 * T + B, False, lambda b: True)
        pass2(kh, 1, 2 * T, 3 * T, False, lambda b: b >= 2 * T + B)
        ret_b[kh].wait_recv()
        send_r[kh, 0] = (dk_s[kh, :T, :] * (SCALE * ok[0]) + recv_b[kh, 0].astype(F32) * odd_f).astype(BF)
        send_r[kh, 1] = (dv_s[kh, :T, :] * ok[0] + recv_b[kh, 1].astype(F32) * odd_f).astype(BF)
        ret_r[kh].start()

    k_sum = jnp.zeros((8, D), F32)
    for kh in range(2):
        for sh in range(3):
            prod = dk_s[kh, sh * T : (sh + 1) * T, :] * kv[sh, kh, 0].astype(F32)
            k_sum = k_sum + jnp.sum(prod.reshape(T // 8, 8, D), axis=0)
    k_sum = jnp.sum(k_sum, axis=0, keepdims=True) * (SCALE / kg)
    for kh in range(2):
        for qb in range(2):
            for h in range(2):
                rows = pl.ds(4 * B * qb + 2 * kh + h, B, stride=4)
                dq_s[rows, :] = jnp.transpose(dq_t[kh, qb, :, h * B : (h + 1) * B]) * SCALE
    q_sum = jnp.sum((dq_s[...] * q_unit[...]).reshape(4 * T // 8, 8, D), axis=0)
    q_sum = jnp.sum(q_sum, axis=0, keepdims=True)
    row8 = lax.broadcasted_iota(jnp.int32, (8, D), 0)
    red_src[0] = jnp.where(row8 == 0, q_sum, jnp.where(row8 == 1, k_sum, 0.0))

    def exchange(level, dst, ssem, rsem, peer, count):
        copies = [
            remote(red_src.at[level], dst.at[d - 1], ssem.at[d - 1], rsem.at[d - 1], peer(d))
            for d in range(1, count)
        ]
        for c in copies:
            c.start()
        return copies

    def absorb(level, dst, copies):
        for c in copies:
            c.wait_recv()
        total = red_src[level]
        for d in range(len(copies)):
            total = total + dst[d]
        red_src[level + 1] = total

    y_copies = exchange(0, red_y, ys_sem, yr_sem, y_peer, n_y)

    def norm_back(grad, unit, inv, gain, out_buf, rows):
        for r in range(0, rows, B):
            u = unit[r : r + B, :]
            du = grad[r : r + B, :] * gain
            m = jnp.mean(du * u, axis=1, keepdims=True)
            out_buf[r : r + B, :] = (inv[r : r + B, :] * (du - u * m)).astype(BF)

    norm_back(dq_s, q_unit, q_inv, qg, q_buf, 4 * T)
    out_q = pltpu.make_async_copy(q_buf, gq_out, out_sem.at[0])
    out_q.start()
    absorb(0, red_y, y_copies)
    z_copies = exchange(1, red_z, zs_sem, zr_sem, z_peer, n_z)

    for kh in range(2):
        ret_r[kh].wait_recv()
        rows = pl.ds(kh, T, stride=2)
        dq_s[rows, :] = (
            dk_s[kh, 2 * T :, :] * SCALE
            + recv_r[kh, 0].astype(F32)
            + recv_b[kh, 0].astype(F32) * even_f
        )
        stage[rows, :] = (
            dv_s[kh, 2 * T :, :] + recv_r[kh, 1].astype(F32) + recv_b[kh, 1].astype(F32) * even_f
        )
    norm_back(dq_s, k_unit, k_inv, kg, k_buf, 2 * T)
    out_k = pltpu.make_async_copy(k_buf, gk_out, out_sem.at[1])
    out_k.start()
    v_buf[...] = stage[: 2 * T, :].astype(BF)
    out_v = pltpu.make_async_copy(v_buf, gv_out, out_sem.at[2])
    out_v.start()
    absorb(1, red_z, z_copies)
    x_copies = exchange(2, red_x, xs_sem, xr_sem, x_peer, n_x)
    absorb(2, red_x, x_copies)
    gain_out[...] = red_src[3]

    for c in y_copies + z_copies + x_copies:
        c.wait_send()
    for kh in range(2):
        fwd[kh].wait_send()
        sib_own[kh].wait_send()
        ret_b[kh].wait_send()
        ret_r[kh].wait_send()
    out_q.wait()
    out_k.wait()
    out_v.wait()


def per_device(n_seq, n_head, query, key, value, grad_out, q_gain, k_gain):
    n_y = Y_HI * Y_LO * CORES
    n_z = n_seq // (CORES * Y_LO)
    n_x = n_head // Y_HI
    hbm = pl.BlockSpec(memory_space=pl.ANY)
    vmem = pl.BlockSpec(memory_space=pltpu.VMEM)
    dma = pltpu.SemaphoreType.DMA
    scratch = [
        pltpu.VMEM((4 * T, D), BF), pltpu.VMEM((4 * T, D), BF),
        pltpu.VMEM((2 * T, D), BF), pltpu.VMEM((2 * T, D), BF),
        pltpu.VMEM((4 * T, D), F32), pltpu.VMEM((4 * T, D), F32),
        pltpu.VMEM((2 * T, D), F32), pltpu.VMEM((2 * T, D), F32),
        pltpu.VMEM((4 * T, D), F32),
        pltpu.VMEM((2, 2, 2 * B, 2 * D), BF), pltpu.VMEM((2, 2, 2 * B, D), BF),
        pltpu.VMEM((2, 2, D, 2 * B), BF), pltpu.VMEM((2, 2, 2 * D, 2 * B), BF),
        pltpu.VMEM((3, 2, 2, T, D), BF),
        pltpu.VMEM((2, KEYS, D), BF),
        pltpu.VMEM((2, D + EXT, KEYS), BF),
        pltpu.VMEM((2, D, KEYS), BF),
        pltpu.VMEM((2, 2, WINDOW + B, 2 * B), BF),
        pltpu.VMEM((WINDOW + B, 2 * B), BF),
        pltpu.VMEM((2, 2, D + EXT, 2 * B), F32),
        pltpu.VMEM((2, 2, D, 2 * B), F32),
        pltpu.VMEM((2, KEYS, D), F32), pltpu.VMEM((2, KEYS, D), F32),
        pltpu.VMEM((4 * T, D), F32),
        pltpu.VMEM((2, 2, T, D), BF), pltpu.VMEM((2, 2, T, D), BF),
        pltpu.VMEM((2, 2, T, D), BF), pltpu.VMEM((2, 2, T, D), BF),
        pltpu.VMEM((4, 8, D), F32),
        pltpu.VMEM((n_y - 1, 8, D), F32),
        pltpu.VMEM((max(n_z - 1, 1), 8, D), F32),
        pltpu.VMEM((max(n_x - 1, 1), 8, D), F32),
        dma((4,)), dma((3,)),
        dma((2,)), dma((2,)), dma((2,)), dma((2,)), dma((2,)), dma((2,)), dma((2,)), dma((2,)),
        dma((n_y - 1,)), dma((n_y - 1,)),
        dma((max(n_z - 1, 1),)), dma((max(n_z - 1, 1),)),
        dma((max(n_x - 1, 1),)), dma((max(n_x - 1, 1),)),
    ]
    gq, gk, gv, gains = pl.pallas_call(
        functools.partial(kernel, (n_seq, n_head)),
        out_shape=(
            jax.ShapeDtypeStruct((4 * T, D), BF),
            jax.ShapeDtypeStruct((2 * T, D), BF),
            jax.ShapeDtypeStruct((2 * T, D), BF),
            jax.ShapeDtypeStruct((8, D), F32),
        ),
        in_specs=[hbm] * 4 + [vmem] * 2,
        out_specs=(hbm, hbm, hbm, vmem),
        scratch_shapes=scratch,
        compiler_params=pltpu.CompilerParams(collective_id=0, has_side_effects=True),
        name="swa_backward",
    )(
        query.reshape(4 * T, D),
        key.reshape(2 * T, D),
        value.reshape(2 * T, D),
        grad_out.reshape(4 * T, D),
        q_gain.reshape(1, D),
        k_gain.reshape(1, D),
    )
    return (
        gq.reshape(T, 4, D),
        gk.reshape(T, 2, D),
        gv.reshape(T, 2, D),
        gains[0],
        gains[1],
    )


def solution(mesh):
    split = P("seq", "head", None)
    return jax.shard_map(
        functools.partial(per_device, mesh.shape["seq"], mesh.shape["head"]),
        mesh=mesh,
        in_specs=(split, split, split, split, P(), P()),
        out_specs=(split, split, split, P(), P()),
        check_vma=False,
    )
```

time: 242 us -> 61.3 us (0.25)
  blocking collectives: 112 us -> 0 us
  Pallas kernels: 0 us -> 54.6 us
  matrix products: 27.7 us -> 0 us
  local copies, waits for them, and re-layouts: 31.5 us -> 5.07 us
  starting transfers between devices: 20.2 us -> 0 us
  waiting for transfers between devices: 19.5 us -> 0 us
  other arithmetic: 18.4 us -> 0 us
  loops' own time: 10.7 us -> 0 us
    psum x1 -> x0, blocking collectives: 112 us -> none  [per_device(): lax.psum((q_gain_part, k_gain_part), ('seq', 'head'))]
    pallas_call x0 -> x1, Pallas kernels: none -> 54.6 us  [per_device(): pl.pallas_call(functools.partial(kernel, (n_seq, n_head)), out_shape=(jax...]
    dot_general x24 -> x0, matrix products: 27.7 us -> none  [the longest x4 6.65 us: head_grads(): lax.dot_general(probs_low, incoming_gradient, first_first, preferred_elem...]
    dynamic_update_slice x4 -> x0, local copies, waits for them, and re-layouts: 23.2 us -> none  [per_device(): lax.scan(per_head, 0, (head_ids, query_heads, upstream_heads))]
    ppermute x8 -> x0, starting transfers between devices: 20.2 us -> none  [passed_along(): lax.ppermute(value, axis, [(source, source + steps) for source in range(i...]
    ppermute x8 -> x0, waiting for transfers between devices: 19.5 us -> none  [passed_along(): lax.ppermute(value, axis, [(source, source + steps) for source in range(i...]
    another operation x1 -> x0, loops' own time: 10.7 us -> none  [per_device(): lax.scan(per_head, 0, (head_ids, query_heads, upstream_heads))]
    reduce_sum x6 -> x0, other arithmetic: 9.5 us -> none  [the longest x2 2.84 us: normalize(): jnp.mean(as_float * as_float, axis=-1, keepdims=True) + norm_eps]
  transfers between devices with their start and end apart: 8 -> 0, of which waited for: 4 -> 0; matrix products, arithmetic and copies ran while one was open for 7% -> 0% of each run, Pallas kernels for 0% -> 0%
where the time goes in v1:
time: 61.3 us; the launch traced here: 60.3 us
  Pallas kernels  54.6 us (89%)
  local copies, waits for them, and re-layouts  5.07 us (8%)
  between operations  0.64 us (1%)
    pallas_call x1, Pallas kernels, per_device(): pl.pallas_call(functools.partial(kernel, (n_seq, n_head)), out_shape=(jax...  54.6 us
    unnamed x7, local copies, waits for them, and re-layouts  3.81 us
    squeeze x1, local copies, waits for them, and re-layouts, per_device(): gains[1]  1.27 us

profile of v1, /device:TPU:1, one launch (start us, length us, event | category | flops | bytes accessed | tf_op | source)
XLA Modules:
  0.0 60.3 jit_solution(12234707434188209963)
XLA Ops:
  0.6 54.6 %swa_backward.1 = (bf16[2048,128]{1,0:T(8,128)(2,1)}, bf16[1024,128]{1,0:T(8,128)(2,1)}, bf16[1024,128]{1,0:T(8,128)(2,1)}, f32[8,128]{1,0:T(8,128)}) custom-call(bf16[2048,128]{1,0:T(8,128)(2,1)} %bitcast.14, bf16[1024,128]{1,0:T(8,128)(2,1)} %bitcast.18, bf16[1024,128]{1,0:T(8,128)(2,1)} %bitcast.19, bf16[2048,128]{1,0:T(8,128)(2,1)} %bitcast.15, ...), custom_call_target="tpu_custom_call" | custom-call | tf_op jit(solution)/shard_map/swa_backward/pallas_call | solution.py:384
  55.2 1.3 %slice_bitcast_fusion = (f32[128]{0:T(128)}, f32[128]{0:T(128)}) fusion(f32[8,128]{1,0:T(8,128)} %get-tuple-element.12), kind=kLoop, calls=%fused_computation | loop fusion | bytes 2048 | tf_op jit(solution)/shard_map/squeeze | solution.py:410
  56.5 0.0 copy-start.1
  56.5 2.1 %copy.14 = bf16[512,4,128]{2,1,0:T(4,128)(2,1)} copy(bf16[512,4,128]{2,1,0:T(4,128)(2,1)} %bitcast.13) | data formatting | bytes 1048576
  58.5 0.0 copy-done.1
  58.5 0.0 copy-start
  58.5 0.7 %copy.15 = bf16[512,2,128]{2,1,0:T(2,128)(2,1)} copy(bf16[512,2,128]{2,1,0:T(2,128)(2,1)S(1)} %bitcast.17) | data formatting | bytes 524288
  59.2 0.3 copy-done
  59.6 0.7 %copy.16 = bf16[512,2,128]{2,1,0:T(2,128)(2,1)} copy(bf16[512,2,128]{2,1,0:T(2,128)(2,1)S(1)} %bitcast.16) | data formatting | bytes 524288
Async XLA Ops:
  56.5 2.1 %copy-start.1 = (bf16[1024,128]{1,0:T(8,128)(2,1)S(1)}, bf16[1024,128]{1,0:T(8,128)(2,1)}, u32[]{:S(2)}) copy-start(bf16[1024,128]{1,0:T(8,128)(2,1)} %get-tuple-element.10) | copy-start | bytes 786436
  58.5 1.0 %copy-start = (bf16[1024,128]{1,0:T(8,128)(2,1)S(1)}, bf16[1024,128]{1,0:T(8,128)(2,1)}, u32[]{:S(2)}) copy-start(bf16[1024,128]{1,0:T(8,128)(2,1)} %get-tuple-element.11) | copy-start | bytes 786436

commit v2 on v1

v2 whole, which is shorter than its diff:
```python
import functools
import math

import jax
import jax.numpy as jnp
from jax import lax
from jax.experimental import pallas as pl
from jax.experimental.pallas import tpu as pltpu
from jax.sharding import PartitionSpec as P

WINDOW = 1024
SCALE = 168.0 ** (-0.5)
EXP2_SCALE = SCALE * math.log2(math.e)
EPS = 1e-06
CORES = 2
Y_LO = 4
Y_HI = 2

BF = jnp.bfloat16
F32 = jnp.float32
MESH = pl.DeviceIdType.MESH

T = 512
D = 128
B = 256
KEYS = 3 * T
EXT = 16


def dot_nn(a, b):
    return lax.dot_general(a, b, (((1,), (0,)), ((), ())), preferred_element_type=F32)


def dot_nt(a, b):
    return lax.dot_general(a, b, (((1,), (1,)), ((), ())), preferred_element_type=F32)


def transposed(x):
    return jnp.transpose(x.astype(F32)).astype(BF)


def kernel(
    sizes,
    q_in, k_in, v_in, g_in, q_gain, k_gain,
    gq_out, gk_out, gv_out, gq_gain_out, gk_gain_out,
    q_buf, g_buf, k_buf, v_buf,
    q_unit, q_inv, k_unit, k_inv, stage,
    q_ext, q_low, g_t, g_ext,
    kv, v_t, k_t, e_s, ds_s, av_s, dq_t,
    dk_s, dv_s, dq_s,
    send_b, recv_b, send_r, recv_r,
    red_src, red_y, red_z, red_x,
    in_sem, up_sem, down_sem,
    f_send, f_recv, s_send, s_recv, b_send, b_recv, r_send, r_recv,
    ys_sem, yr_sem, zs_sem, zr_sem, xs_sem, xr_sem,
):
    n_seq, n_head = sizes
    n_z = n_seq // (CORES * Y_LO)
    n_x = n_head // Y_HI
    n_y = Y_HI * Y_LO * CORES
    seq = lax.axis_index("seq")
    head = lax.axis_index("head")
    core = lax.rem(seq, CORES)
    y_lo = lax.rem(lax.div(seq, CORES), Y_LO)
    z = lax.div(seq, CORES * Y_LO)
    x = lax.rem(head, n_x)
    y_hi = lax.div(head, n_x)
    y_rank = (y_hi * Y_LO + y_lo) * CORES + core
    ahead = (seq + 2, head)
    behind = (seq - 2, head)
    sibling = (seq + 1 - 2 * core, head)
    z_step = CORES * Y_LO
    above = (seq + z_step, head)
    below = (seq - z_step, head)
    is_odd = core == 1
    is_even = core == 0
    has_ahead = seq < n_seq - 2
    has_behind = seq >= 2
    has_above = z < n_z - 1
    has_below = z > 0

    def y_peer(d):
        r = lax.rem(y_rank + d, n_y)
        c = lax.rem(r, CORES)
        yl = lax.rem(lax.div(r, CORES), Y_LO)
        yh = lax.div(r, CORES * Y_LO)
        return ((z * Y_LO + yl) * CORES + c, yh * n_x + x)

    def z_peer(d):
        return ((lax.rem(z + d, n_z) * Y_LO + y_lo) * CORES + core, head)

    def x_peer(d):
        return (seq, y_hi * n_x + lax.rem(x + d, n_x))

    def signal(sem, dev):
        pl.semaphore_signal(sem, inc=1, device_id=dev, device_id_type=MESH)

    def remote(src, dst, ssem, rsem, dev):
        return pltpu.make_async_remote_copy(
            src_ref=src, dst_ref=dst, send_sem=ssem, recv_sem=rsem, device_id=dev, device_id_type=MESH
        )

    ins = [
        pltpu.make_async_copy(src, dst, in_sem.at[i])
        for i, (src, dst) in enumerate(
            ((k_in, k_buf), (v_in, v_buf), (q_in, q_buf), (g_in, g_buf))
        )
    ]
    for c in ins:
        c.start()

    barrier = pltpu.get_barrier_semaphore()
    always = [y_peer(d) for d in range(1, n_y)] + [x_peer(d) for d in range(1, n_x)]
    for p in always:
        signal(barrier, p)
    sometimes = ((has_ahead, ahead), (has_behind, behind), (has_above, above), (has_below, below))
    expected = jnp.int32(len(always))
    for there, p in sometimes:
        expected = expected + there.astype(jnp.int32)

        @pl.when(there)
        def _(p=p):
            signal(barrier, p)

    ok = [has_behind.astype(F32), (seq >= 1).astype(F32), jnp.float32(1.0)]

    @pl.when(jnp.logical_not(has_behind))
    def _():
        kv[0] = jnp.zeros((2, 2, T, D), BF)

    @pl.when(seq == 0)
    def _():
        kv[1] = jnp.zeros((2, 2, T, D), BF)

    @pl.when(jnp.logical_not(has_ahead))
    def _():
        recv_r[...] = jnp.zeros((2, 2, T, D), BF)

    def normalise(buf, unit, inv, rows):
        for r in range(0, rows, B):
            f = buf[r : r + B, :].astype(F32)
            i = lax.rsqrt(jnp.mean(f * f, axis=1, keepdims=True) + EPS)
            unit[r : r + B, :] = f * i
            inv[r : r + B, :] = jnp.broadcast_to(i, (B, D))

    kg = k_gain[...]
    qg = q_gain[...]
    ins[0].wait()
    normalise(k_buf, k_unit, k_inv, 2 * T)
    ins[1].wait()
    stage[: 2 * T, :] = v_buf[...].astype(F32)
    for kh in range(2):
        kv[2, kh, 0] = (k_unit[pl.ds(kh, T, stride=2), :] * kg).astype(BF)
        kv[2, kh, 1] = stage[pl.ds(kh, T, stride=2), :].astype(BF)
    pl.semaphore_wait(barrier, expected)

    parts = [(kh, i) for kh in range(2) for i in range(2)]
    fwd = {p: remote(kv.at[2, *p], kv.at[0, *p], f_send.at[*p], f_recv.at[*p], ahead) for p in parts}
    sib_own = {p: remote(kv.at[2, *p], kv.at[1, *p], s_send.at[*p], s_recv.at[*p], sibling) for p in parts}
    sib_fwd = {p: remote(kv.at[0, *p], kv.at[1, *p], s_send.at[*p], s_recv.at[*p], sibling) for p in parts}
    ret_b = [remote(send_b.at[kh], recv_b.at[kh], b_send.at[kh], b_recv.at[kh], sibling) for kh in range(2)]
    ret_r = [remote(send_r.at[kh], recv_r.at[kh], r_send.at[kh], r_recv.at[kh], behind) for kh in range(2)]

    @pl.when(has_ahead)
    def _():
        for p in parts:
            fwd[p].start()

    @pl.when(is_even)
    def _():
        for p in parts:
            sib_own[p].start()

    @pl.when(jnp.logical_not(has_below))
    def _():
        signal(up_sem, above)

    @pl.when(jnp.logical_not(has_above))
    def _():
        signal(down_sem, below)

    def pass_up():
        @pl.when(has_below)
        def _():
            pl.semaphore_wait(up_sem, 1)

            @pl.when(has_above)
            def _():
                signal(up_sem, above)

    def pass_down(low, high):
        @pl.when(has_above & (z >= low) & (z < high))
        def _():
            pl.semaphore_wait(down_sem, 1)

            @pl.when(has_below)
            def _():
                signal(down_sem, below)

    def rows_of(kh, qb, h):
        return pl.ds(4 * B * qb + 2 * kh + h, B, stride=4)

    ins[2].wait()
    normalise(q_buf, q_unit, q_inv, 4 * T)
    ins[3].wait()
    stage[...] = g_buf[...].astype(F32)
    for kh in range(2):
        for qb in range(2):
            for h in range(2):
                rows = rows_of(kh, qb, h)
                low = (q_unit[rows, :] * qg).astype(BF)
                scaled = low.astype(F32) * EXP2_SCALE
                high = scaled.astype(BF)
                rest = (scaled - high.astype(F32)).astype(BF)
                at = slice(h * B, (h + 1) * B)
                q_low[kh, qb, at, :] = low
                q_ext[kh, qb, at, :D] = high
                q_ext[kh, qb, at, D:] = rest
                g_t[kh, qb, :, at] = jnp.transpose(stage[rows, :]).astype(BF)
    pass_up()
    pass_down(n_z - 3, n_z)

    def prepare_k(sh, kh):
        k_t[kh, :, sh * T : (sh + 1) * T] = transposed(kv[sh, kh, 0])

    def prepare_v(sh, kh):
        span = slice(sh * T, (sh + 1) * T)
        v_t[kh, :D, span] = transposed(kv[sh, kh, 1])
        v_t[kh, D:, span] = jnp.full((EXT, T), ok[sh], F32).astype(BF)

    key_row = lax.broadcasted_iota(jnp.int32, (B, 2 * B), 0)
    query_col = lax.rem(lax.broadcasted_iota(jnp.int32, (B, 2 * B), 1), B)

    def weigh(kh, qb, r0, r1):
        off = qb * B
        for b in range(r0, r1, B):
            k = kv[b // T, kh, 0, b % T : b % T + B, :]
            s = dot_nt(jnp.concatenate([k, k], axis=1), q_ext[kh, qb])
            e = jnp.exp2(s)
            if b == off:
                e = jnp.where(key_row > query_col, e, 0.0)
            if b == off + WINDOW:
                e = jnp.where(key_row <= query_col, e, 0.0)
            e_s[kh, qb, b - off : b - off + B, :] = e.astype(BF)

    def attend(kh, qb, r0, r1, first):
        off = qb * B
        av = dot_nn(v_t[kh, :, r0:r1], e_s[kh, qb, r0 - off : r1 - off, :])
        if first:
            av_s[kh, qb] = av
        else:
            av_s[kh, qb] += av

    def finish(kh, qb):
        l_row = av_s[kh, qb, D : D + 1, :]
        inv = 1.0 / l_row
        scaled = (g_t[kh, qb].astype(F32) * inv).astype(BF)
        g_ext[kh, qb, :D, :] = scaled
        off = -inv * jnp.sum(scaled.astype(F32) * av_s[kh, qb, :D, :], axis=0, keepdims=True)
        high = off.astype(BF).astype(F32)
        rest = off - high
        row = lax.broadcasted_iota(jnp.int32, (EXT, 2 * B), 0)
        tail = jnp.where(row == 0, high, jnp.where(row == 1, rest, 0.0))
        g_ext[kh, qb, D : D + EXT, :] = tail.astype(BF)
        g_ext[kh, qb, D + EXT :, :] = jnp.zeros((D - EXT, 2 * B), BF)

    def grads(kh, qb, r0, r1, first_q, first_of):
        off = qb * B
        for b in range(r0, r1, B):
            sh = b // T
            ones = jnp.full((B, D), ok[sh], F32).astype(BF)
            vx = jnp.concatenate([kv[sh, kh, 1, b % T : b % T + B, :], ones], axis=1)
            dp = dot_nn(vx, g_ext[kh, qb])
            e = e_s[kh, qb, b - off : b - off + B, :]
            ds = e * dp.astype(BF)
            ds_s[b - off : b - off + B, :] = ds
            dv = dot_nt(e, g_ext[kh, qb, :D, :])
            dk = dot_nn(ds, q_low[kh, qb])
            if first_of(b):
                dv_s[kh, b : b + B, :] = dv
                dk_s[kh, b : b + B, :] = dk
            else:
                dv_s[kh, b : b + B, :] += dv
                dk_s[kh, b : b + B, :] += dk
        dq = dot_nn(k_t[kh, :, r0:r1], ds_s[r0 - off : r1 - off, :])
        if first_q:
            dq_t[kh, qb] = dq
        else:
            dq_t[kh, qb] += dq

    for kh in range(2):
        prepare_k(2, kh)
        weigh(kh, 0, 2 * T, 2 * T + B)
        weigh(kh, 1, 2 * T, 3 * T)
    for kh in range(2):
        prepare_v(2, kh)
        attend(kh, 0, 2 * T, 2 * T + B, True)
        attend(kh, 1, 2 * T, 3 * T, True)

    odd_f = is_odd.astype(F32)
    even_f = is_even.astype(F32)

    def take(p):
        @pl.when(has_behind)
        def _():
            fwd[p].wait_recv()

            @pl.when(is_odd)
            def _():
                sib_fwd[p].start()

    def take_b(p):
        @pl.when(seq >= 1)
        def _():
            sib_own[p].wait_recv()

    def pay_back(kh):
        ret_b[kh].wait_recv()
        send_r[kh, 0] = (dk_s[kh, :T, :] * SCALE + recv_b[kh, 0].astype(F32) * odd_f).astype(BF)
        send_r[kh, 1] = (dv_s[kh, :T, :] + recv_b[kh, 1].astype(F32) * odd_f).astype(BF)

        @pl.when(has_behind)
        def _():
            ret_r[kh].start()

    q_sum = jnp.zeros((8, D), F32)
    k_sum = jnp.zeros((8, D), F32)
    for kh in range(2):
        if kh == 0:
            take((0, 0))
        prepare_k(0, kh)
        take_b((kh, 0))
        prepare_k(1, kh)
        weigh(kh, 0, 0, 2 * T)
        weigh(kh, 1, B, 2 * T)
        take((kh, 1))
        prepare_v(0, kh)
        take_b((kh, 1))
        prepare_v(1, kh)
        attend(kh, 0, 0, 2 * T, False)
        attend(kh, 1, B, 2 * T, False)
        finish(kh, 0)
        finish(kh, 1)
        grads(kh, 0, 0, 2 * T, True, lambda b: True)
        grads(kh, 1, B, 2 * T, True, lambda b: False)
        send_b[kh, 0] = (dk_s[kh, T : 2 * T, :] * SCALE).astype(BF)
        send_b[kh, 1] = dv_s[kh, T : 2 * T, :].astype(BF)
        ret_b[kh].start()
        if kh == 0:
            take((1, 0))
        grads(kh, 0, 2 * T, 2 * T + B, False, lambda b: True)
        grads(kh, 1, 2 * T, 3 * T, False, lambda b: b >= 2 * T + B)
        for sh in range(3):
            prod = dk_s[kh, sh * T : (sh + 1) * T, :] * kv[sh, kh, 0].astype(F32)
            k_sum = k_sum + jnp.sum(prod.reshape(T // 8, 8, D), axis=0)
        for qb in range(2):
            for h in range(2):
                rows = rows_of(kh, qb, h)
                dq = jnp.transpose(dq_t[kh, qb, :, h * B : (h + 1) * B]) * SCALE
                dq_s[rows, :] = dq
                q_sum = q_sum + jnp.sum((dq * q_unit[rows, :]).reshape(B // 8, 8, D), axis=0)
        if kh == 0:
            pay_back(0)
            pass_down(n_z - 5, n_z - 3)
    pass_down(0, n_z - 5)

    k_row = jnp.sum(k_sum, axis=0, keepdims=True) * (SCALE / kg)
    q_row = jnp.sum(q_sum, axis=0, keepdims=True)
    row8 = lax.broadcasted_iota(jnp.int32, (8, D), 0)
    red_src[0] = jnp.where(row8 == 0, q_row, jnp.where(row8 == 1, k_row, 0.0))

    def exchange(level, dst, ssem, rsem, peer, count):
        copies = [
            remote(red_src.at[level], dst.at[d - 1], ssem.at[d - 1], rsem.at[d - 1], peer(d))
            for d in range(1, count)
        ]
        for c in copies:
            c.start()
        return copies

    def absorb(level, dst, copies):
        for c in copies:
            c.wait_recv()
        total = red_src[level]
        for d in range(len(copies)):
            total = total + dst[d]
        red_src[level + 1] = total

    y_copies = exchange(0, red_y, ys_sem, yr_sem, y_peer, n_y)
    pay_back(1)

    def norm_back(grad, unit, inv, gain, out, rows):
        for r in range(0, rows, B):
            u = unit[r : r + B, :]
            du = grad[r : r + B, :] * gain
            m = jnp.mean(du * u, axis=1, keepdims=True)
            out[r : r + B, :] = (inv[r : r + B, :] * (du - u * m)).astype(BF)

    absorb(0, red_y, y_copies)
    z_copies = exchange(1, red_z, zs_sem, zr_sem, z_peer, n_z)
    norm_back(dq_s, q_unit, q_inv, qg, gq_out, 4 * T)
    absorb(1, red_z, z_copies)
    x_copies = exchange(2, red_x, xs_sem, xr_sem, x_peer, n_x)

    for kh in range(2):

        @pl.when(has_ahead)
        def _(kh=kh):
            ret_r[kh].wait_recv()

        rows = pl.ds(kh, T, stride=2)
        dq_s[rows, :] = (
            dk_s[kh, 2 * T :, :] * SCALE
            + recv_r[kh, 0].astype(F32)
            + recv_b[kh, 0].astype(F32) * even_f
        )
        stage[rows, :] = (
            dv_s[kh, 2 * T :, :] + recv_r[kh, 1].astype(F32) + recv_b[kh, 1].astype(F32) * even_f
        )
    norm_back(dq_s, k_unit, k_inv, kg, gk_out, 2 * T)
    gv_out[...] = stage[: 2 * T, :].astype(BF)
    absorb(2, red_x, x_copies)
    gq_gain_out[...] = red_src[3, 0:1, :]
    gk_gain_out[...] = red_src[3, 1:2, :]

    for c in y_copies + z_copies + x_copies + ret_b:
        c.wait_send()

    @pl.when(has_ahead)
    def _():
        for p in parts:
            fwd[p].wait_send()

    @pl.when(is_even | has_behind)
    def _():
        for p in parts:
            sib_own[p].wait_send()

    @pl.when(has_behind)
    def _():
        for kh in range(2):
            ret_r[kh].wait_send()


def write_out(*refs):
    sem = refs[-1]
    n = (len(refs) - 1) // 2
    copies = [pltpu.make_async_copy(refs[i], refs[n + i], sem.at[i]) for i in range(n)]
    for c in copies:
        c.start()
    for c in copies:
        c.wait()


def per_device(n_seq, n_head, query, key, value, grad_out, q_gain, k_gain):
    n_y = Y_HI * Y_LO * CORES
    n_z = n_seq // (CORES * Y_LO)
    n_x = n_head // Y_HI
    hbm = pl.BlockSpec(memory_space=pl.ANY)
    vmem = pl.BlockSpec(memory_space=pltpu.VMEM)
    dma = pltpu.SemaphoreType.DMA
    scratch = [
        pltpu.VMEM((4 * T, D), BF), pltpu.VMEM((4 * T, D), BF),
        pltpu.VMEM((2 * T, D), BF), pltpu.VMEM((2 * T, D), BF),
        pltpu.VMEM((4 * T, D), F32), pltpu.VMEM((4 * T, D), F32),
        pltpu.VMEM((2 * T, D), F32), pltpu.VMEM((2 * T, D), F32),
        pltpu.VMEM((4 * T, D), F32),
        pltpu.VMEM((2, 2, 2 * B, 2 * D), BF), pltpu.VMEM((2, 2, 2 * B, D), BF),
        pltpu.VMEM((2, 2, D, 2 * B), BF), pltpu.VMEM((2, 2, 2 * D, 2 * B), BF),
        pltpu.VMEM((3, 2, 2, T, D), BF),
        pltpu.VMEM((2, D + EXT, KEYS), BF),
        pltpu.VMEM((2, D, KEYS), BF),
        pltpu.VMEM((2, 2, WINDOW + B, 2 * B), BF),
        pltpu.VMEM((WINDOW + B, 2 * B), BF),
        pltpu.VMEM((2, 2, D + EXT, 2 * B), F32),
        pltpu.VMEM((2, 2, D, 2 * B), F32),
        pltpu.VMEM((2, KEYS, D), F32), pltpu.VMEM((2, KEYS, D), F32),
        pltpu.VMEM((4 * T, D), F32),
        pltpu.VMEM((2, 2, T, D), BF), pltpu.VMEM((2, 2, T, D), BF),
        pltpu.VMEM((2, 2, T, D), BF), pltpu.VMEM((2, 2, T, D), BF),
        pltpu.VMEM((4, 8, D), F32),
        pltpu.VMEM((n_y - 1, 8, D), F32),
        pltpu.VMEM((max(n_z - 1, 1), 8, D), F32),
        pltpu.VMEM((max(n_x - 1, 1), 8, D), F32),
        dma((4,)), pltpu.SemaphoreType.REGULAR, pltpu.SemaphoreType.REGULAR,
        dma((2, 2)), dma((2, 2)), dma((2, 2)), dma((2, 2)), dma((2,)), dma((2,)), dma((2,)), dma((2,)),
        dma((n_y - 1,)), dma((n_y - 1,)),
        dma((max(n_z - 1, 1),)), dma((max(n_z - 1, 1),)),
        dma((max(n_x - 1, 1),)), dma((max(n_x - 1, 1),)),
    ]
    shapes = [((4 * T, D), BF), ((2 * T, D), BF), ((2 * T, D), BF), ((1, D), F32), ((1, D), F32)]
    held = pl.pallas_call(
        functools.partial(kernel, (n_seq, n_head)),
        out_shape=[pltpu.VMEM(*s) for s in shapes],
        in_specs=[hbm] * 4 + [vmem] * 2,
        out_specs=[vmem] * len(shapes),
        scratch_shapes=scratch,
        compiler_params=pltpu.CompilerParams(collective_id=0, has_side_effects=True),
        name="swa_backward",
    )(
        query.reshape(4 * T, D),
        key.reshape(2 * T, D),
        value.reshape(2 * T, D),
        grad_out.reshape(4 * T, D),
        q_gain.reshape(1, D),
        k_gain.reshape(1, D),
    )
    gq, gk, gv, gq_gain, gk_gain = pl.pallas_call(
        write_out,
        out_shape=[jax.ShapeDtypeStruct(*s) for s in shapes],
        in_specs=[vmem] * len(shapes),
        out_specs=[hbm] * len(shapes),
        scratch_shapes=[dma((len(shapes),))],
        name="write_out",
    )(*[pltpu.with_memory_space_constraint(a, pltpu.VMEM) for a in held])
    return (
        gq.reshape(T, 4, D),
        gk.reshape(T, 2, D),
        gv.reshape(T, 2, D),
        gq_gain.reshape(D),
        gk_gain.reshape(D),
    )


def solution(mesh):
    split = P("seq", "head", None)
    return jax.shard_map(
        functools.partial(per_device, mesh.shape["seq"], mesh.shape["head"]),
        mesh=mesh,
        in_specs=(split, split, split, split, P(), P()),
        out_specs=(split, split, split, P(), P()),
        check_vma=False,
    )
```

time: 61.3 us -> 54.2 us (0.88)
  local copies, waits for them, and re-layouts: 5.07 us -> 0 us
  Pallas kernels: 54.6 us -> 53.1 us
    unnamed x7 -> x0, local copies, waits for them, and re-layouts: 3.81 us -> none
    pallas_call x1 -> x2, Pallas kernels: 54.6 us -> 53.1 us  [the longest x1 52 us: per_device(): pl.pallas_call(functools.partial(kernel, (n_seq, n_head)), out_shape=[plt...]
    squeeze x1 -> x0, local copies, waits for them, and re-layouts: 1.27 us -> none  [per_device(): gains[1]]
where the time goes in v2:
time: 54.2 us; the launch traced here: 53.7 us
  Pallas kernels  53.1 us (98%)
  between operations  0.64 us (1%)
    pallas_call x1, Pallas kernels, per_device(): pl.pallas_call(functools.partial(kernel, (n_seq, n_head)), out_shape=[plt...  52 us

profile of v2, /device:TPU:1, one launch (start us, length us, event | category | flops | bytes accessed | tf_op | source)
XLA Modules:
  0.0 53.7 jit_solution(2871345125077808878)
XLA Ops:
  0.6 52.0 %swa_backward.1 = (bf16[2048,128]{1,0:T(8,128)(2,1)S(1)}, bf16[1024,128]{1,0:T(8,128)(2,1)S(1)}, bf16[1024,128]{1,0:T(8,128)(2,1)S(1)}, f32[1,128]{1,0:T(1,128)S(1)}, f32[1,128]{1,0:T(1,128)S(1)}) custom-call(bf16[2048,128]{1,0:T(8,128)(2,1)} %bitcast.11, bf16[1024,128]{1,0:T(8,128)(2,1)} %bitcast.13, bf16[1024,128]{1,0:T(8,128)(2,1)} %bitcast.14, ...), custom_call_target="tpu_custom_call" | custom-call | tf_op jit(solution)/shard_map/swa_backward/pallas_call | solution.py:492
  52.7 1.0 %write_out.1 = (bf16[2048,128]{1,0:T(8,128)(2,1)}, bf16[1024,128]{1,0:T(8,128)(2,1)}, bf16[1024,128]{1,0:T(8,128)(2,1)}, f32[1,128]{1,0:T(1,128)}, f32[1,128]{1,0:T(1,128)}) custom-call(bf16[2048,128]{1,0:T(8,128)(2,1)S(1)} %get-tuple-element.15.refs_0_, bf16[1024,128]{1,0:T(8,128)(2,1)S(1)} %get-tuple-element.16.refs_1_, ...), custom_call_target="tpu_custom_call" | custom-call | tf_op jit(solution)/shard_map/write_out/pallas_call | solution.py:508

commit v3 on v2

--- a/solution.py
+++ b/solution.py
@@ -46,7 +46,7 @@
     q_buf, g_buf, k_buf, v_buf,
     q_unit, q_inv, k_unit, k_inv, stage,
     q_ext, q_low, g_t, g_ext,
-    kv, v_t, k_t, e_s, ds_s, av_s, dq_t,
+    k_raw, kv, v_t, k_t, e_s, ds_s, av_s, dq_t,
     dk_s, dv_s, dq_s,
     send_b, recv_b, send_r, recv_r,
     red_src, red_y, red_z, red_x,
@@ -126,10 +126,12 @@
 
     @pl.when(jnp.logical_not(has_behind))
     def _():
+        k_raw[0] = jnp.zeros((2 * T, D), BF)
         kv[0] = jnp.zeros((2, 2, T, D), BF)
 
     @pl.when(seq == 0)
     def _():
+        k_raw[1] = jnp.zeros((2 * T, D), BF)
         kv[1] = jnp.zeros((2, 2, T, D), BF)
 
     @pl.when(jnp.logical_not(has_ahead))
@@ -145,31 +147,38 @@
 
     kg = k_gain[...]
     qg = q_gain[...]
-    ins[0].wait()
-    normalise(k_buf, k_unit, k_inv, 2 * T)
+    def pieces(sh, own):
+        return [k_in if own else k_raw.at[sh]] + [kv.at[2 if own else sh, kh, 1] for kh in range(2)]
+
+    def hop(own, sh, ssem, rsem, dev):
+        return [
+            remote(src, dst, ssem.at[i], rsem.at[i], dev)
+            for i, (src, dst) in enumerate(zip(pieces(0, own), pieces(sh, False)))
+        ]
+
+    fwd = hop(True, 0, f_send, f_recv, ahead)
+    sib_own = hop(True, 1, s_send, s_recv, sibling)
+    sib_fwd = hop(False, 1, s_send, s_recv, sibling)
+    ret_b = [remote(send_b.at[kh], recv_b.at[kh], b_send.at[kh], b_recv.at[kh], sibling) for kh in range(2)]
+    ret_r = [remote(send_r.at[kh], recv_r.at[kh], r_send.at[kh], r_recv.at[kh], behind) for kh in range(2)]
+
+    def give(i):
+        @pl.when(has_ahead)
+        def _():
+            fwd[i].start()
+
+        @pl.when(is_even)
+        def _():
+            sib_own[i].start()
+
+    pl.semaphore_wait(barrier, expected)
+    give(0)
     ins[1].wait()
     stage[: 2 * T, :] = v_buf[...].astype(F32)
     for kh in range(2):
-        kv[2, kh, 0] = (k_unit[pl.ds(kh, T, stride=2), :] * kg).astype(BF)
         kv[2, kh, 1] = stage[pl.ds(kh, T, stride=2), :].astype(BF)
-    pl.semaphore_wait(barrier, expected)
-
-    parts = [(kh, i) for kh in range(2) for i in range(2)]
-    fwd = {p: remote(kv.at[2, *p], kv.at[0, *p], f_send.at[*p], f_recv.at[*p], ahead) for p in parts}
-    sib_own = {p: remote(kv.at[2, *p], kv.at[1, *p], s_send.at[*p], s_recv.at[*p], sibling) for p in parts}
-    sib_fwd = {p: remote(kv.at[0, *p], kv.at[1, *p], s_send.at[*p], s_recv.at[*p], sibling) for p in parts}
-    ret_b = [remote(send_b.at[kh], recv_b.at[kh], b_send.at[kh], b_recv.at[kh], sibling) for kh in range(2)]
-    ret_r = [remote(send_r.at[kh], recv_r.at[kh], r_send.at[kh], r_recv.at[kh], behind) for kh in range(2)]
-
-    @pl.when(has_ahead)
-    def _():
-        for p in parts:
-            fwd[p].start()
-
-    @pl.when(is_even)
-    def _():
-        for p in parts:
-            sib_own[p].start()
+    give(1)
+    give(2)
 
     @pl.when(jnp.logical_not(has_below))
     def _():
@@ -200,6 +209,10 @@
     def rows_of(kh, qb, h):
         return pl.ds(4 * B * qb + 2 * kh + h, B, stride=4)
 
+    ins[0].wait()
+    normalise(k_buf, k_unit, k_inv, 2 * T)
+    for kh in range(2):
+        kv[2, kh, 0] = (k_unit[pl.ds(kh, T, stride=2), :] * kg).astype(BF)
     ins[2].wait()
     normalise(q_buf, q_unit, q_inv, 4 * T)
     ins[3].wait()
@@ -220,8 +233,16 @@
     pass_up()
     pass_down(n_z - 3, n_z)
 
-    def prepare_k(sh, kh):
-        k_t[kh, :, sh * T : (sh + 1) * T] = transposed(kv[sh, kh, 0])
+    def prepare_k(sh):
+        if sh < 2:
+            for r in range(0, 2 * T, B):
+                f = k_raw[sh, r : r + B, :].astype(F32)
+                i = lax.rsqrt(jnp.mean(f * f, axis=1, keepdims=True) + EPS)
+                stage[r : r + B, :] = f * i * kg
+        for kh in range(2):
+            if sh < 2:
+                kv[sh, kh, 0] = stage[pl.ds(kh, T, stride=2), :].astype(BF)
+            k_t[kh, :, sh * T : (sh + 1) * T] = transposed(kv[sh, kh, 0])
 
     def prepare_v(sh, kh):
         span = slice(sh * T, (sh + 1) * T)
@@ -288,8 +309,8 @@
         else:
             dq_t[kh, qb] += dq
 
-    for kh in range(2):
-        prepare_k(2, kh)
+    prepare_k(2)
+    for kh in range(2):
         weigh(kh, 0, 2 * T, 2 * T + B)
         weigh(kh, 1, 2 * T, 3 * T)
     for kh in range(2):
@@ -323,19 +344,21 @@
         def _():
             ret_r[kh].start()
 
+    take(0)
+    prepare_k(0)
+    take_b(0)
+    prepare_k(1)
+    for kh in range(2):
+        weigh(kh, 0, 0, 2 * T)
+        weigh(kh, 1, B, 2 * T)
+
     q_sum = jnp.zeros((8, D), F32)
     k_sum = jnp.zeros((8, D), F32)
     for kh in range(2):
         if kh == 0:
-            take((0, 0))
-        prepare_k(0, kh)
-        take_b((kh, 0))
-        prepare_k(1, kh)
-        weigh(kh, 0, 0, 2 * T)
-        weigh(kh, 1, B, 2 * T)
-        take((kh, 1))
+            take(1)
         prepare_v(0, kh)
-        take_b((kh, 1))
+        take_b(1 + kh)
         prepare_v(1, kh)
         attend(kh, 0, 0, 2 * T, False)
         attend(kh, 1, B, 2 * T, False)
@@ -347,7 +370,7 @@
         send_b[kh, 1] = dv_s[kh, T : 2 * T, :].astype(BF)
         ret_b[kh].start()
         if kh == 0:
-            take((1, 0))
+            take(2)
         grads(kh, 0, 2 * T, 2 * T + B, False, lambda b: True)
         grads(kh, 1, 2 * T, 3 * T, False, lambda b: b >= 2 * T + B)
         for sh in range(3):
@@ -366,8 +389,7 @@
 
     k_row = jnp.sum(k_sum, axis=0, keepdims=True) * (SCALE / kg)
     q_row = jnp.sum(q_sum, axis=0, keepdims=True)
-    row8 = lax.broadcasted_iota(jnp.int32, (8, D), 0)
-    red_src[0] = jnp.where(row8 == 0, q_row, jnp.where(row8 == 1, k_row, 0.0))
+    red_src[0] = jnp.concatenate([q_row, k_row], axis=0)
 
     def exchange(level, dst, ssem, rsem, peer, count):
         copies = [
@@ -386,9 +408,6 @@
             total = total + dst[d]
         red_src[level + 1] = total
 
-    y_copies = exchange(0, red_y, ys_sem, yr_sem, y_peer, n_y)
-    pay_back(1)
-
     def norm_back(grad, unit, inv, gain, out, rows):
         for r in range(0, rows, B):
             u = unit[r : r + B, :]
@@ -396,11 +415,13 @@
             m = jnp.mean(du * u, axis=1, keepdims=True)
             out[r : r + B, :] = (inv[r : r + B, :] * (du - u * m)).astype(BF)
 
-    absorb(0, red_y, y_copies)
-    z_copies = exchange(1, red_z, zs_sem, zr_sem, z_peer, n_z)
+    z_copies = exchange(0, red_z, zs_sem, zr_sem, z_peer, n_z)
+    pay_back(1)
     norm_back(dq_s, q_unit, q_inv, qg, gq_out, 4 * T)
-    absorb(1, red_z, z_copies)
-    x_copies = exchange(2, red_x, xs_sem, xr_sem, x_peer, n_x)
+    absorb(0, red_z, z_copies)
+    x_copies = exchange(1, red_x, xs_sem, xr_sem, x_peer, n_x)
+    absorb(1, red_x, x_copies)
+    y_copies = exchange(2, red_y, ys_sem, yr_sem, y_peer, n_y)
 
     for kh in range(2):
 
@@ -419,7 +440,7 @@
         )
     norm_back(dq_s, k_unit, k_inv, kg, gk_out, 2 * T)
     gv_out[...] = stage[: 2 * T, :].astype(BF)
-    absorb(2, red_x, x_copies)
+    absorb(2, red_y, y_copies)
     gq_gain_out[...] = red_src[3, 0:1, :]
     gk_gain_out[...] = red_src[3, 1:2, :]
 
@@ -428,13 +449,13 @@
 
     @pl.when(has_ahead)
     def _():
-        for p in parts:
-            fwd[p].wait_send()
+        for c in fwd:
+            c.wait_send()
 
     @pl.when(is_even | has_behind)
     def _():
-        for p in parts:
-            sib_own[p].wait_send()
+        for c in sib_own:
+            c.wait_send()
 
     @pl.when(has_behind)
     def _():
@@ -467,6 +488,7 @@
         pltpu.VMEM((4 * T, D), F32),
         pltpu.VMEM((2, 2, 2 * B, 2 * D), BF), pltpu.VMEM((2, 2, 2 * B, D), BF),
         pltpu.VMEM((2, 2, D, 2 * B), BF), pltpu.VMEM((2, 2, 2 * D, 2 * B), BF),
+        pltpu.VMEM((2, 2 * T, D), BF),
         pltpu.VMEM((3, 2, 2, T, D), BF),
         pltpu.VMEM((2, D + EXT, KEYS), BF),
         pltpu.VMEM((2, D, KEYS), BF),
@@ -478,12 +500,12 @@
         pltpu.VMEM((4 * T, D), F32),
         pltpu.VMEM((2, 2, T, D), BF), pltpu.VMEM((2, 2, T, D), BF),
         pltpu.VMEM((2, 2, T, D), BF), pltpu.VMEM((2, 2, T, D), BF),
-        pltpu.VMEM((4, 8, D), F32),
-        pltpu.VMEM((n_y - 1, 8, D), F32),
-        pltpu.VMEM((max(n_z - 1, 1), 8, D), F32),
-        pltpu.VMEM((max(n_x - 1, 1), 8, D), F32),
+        pltpu.VMEM((4, 2, D), F32),
+        pltpu.VMEM((n_y - 1, 2, D), F32),
+        pltpu.VMEM((max(n_z - 1, 1), 2, D), F32),
+        pltpu.VMEM((max(n_x - 1, 1), 2, D), F32),
         dma((4,)), pltpu.SemaphoreType.REGULAR, pltpu.SemaphoreType.REGULAR,
-        dma((2, 2)), dma((2, 2)), dma((2, 2)), dma((2, 2)), dma((2,)), dma((2,)), dma((2,)), dma((2,)),
+        dma((3,)), dma((3,)), dma((3,)), dma((3,)), dma((2,)), dma((2,)), dma((2,)), dma((2,)),
         dma((n_y - 1,)), dma((n_y - 1,)),
         dma((max(n_z - 1, 1),)), dma((max(n_z - 1, 1),)),
         dma((max(n_x - 1, 1),)), dma((max(n_x - 1, 1),)),

time: 54.2 us -> 51.2 us (0.945)
  Pallas kernels: 53.1 us -> 50.4 us
    pallas_call x1, Pallas kernels: 52 us -> 49.4 us  [per_device(): pl.pallas_call(functools.partial(kernel, (n_seq, n_head)), out_shape=[plt...]
where the time goes in v3:
time: 51.2 us; the launch traced here: 51 us
  Pallas kernels  50.4 us (98%)
  between operations  0.64 us (1%)
    pallas_call x1, Pallas kernels, per_device(): pl.pallas_call(functools.partial(kernel, (n_seq, n_head)), out_shape=[plt...  49.4 us

profile of v3, /device:TPU:1, one launch (start us, length us, event | category | flops | bytes accessed | tf_op | source)
XLA Modules:
  0.0 51.0 jit_solution(2623656418694633997)
XLA Ops:
  0.6 49.4 %swa_backward.1 = (bf16[2048,128]{1,0:T(8,128)(2,1)S(1)}, bf16[1024,128]{1,0:T(8,128)(2,1)S(1)}, bf16[1024,128]{1,0:T(8,128)(2,1)S(1)}, f32[1,128]{1,0:T(1,128)S(1)}, f32[1,128]{1,0:T(1,128)S(1)}) custom-call(bf16[2048,128]{1,0:T(8,128)(2,1)} %bitcast.11, bf16[1024,128]{1,0:T(8,128)(2,1)} %bitcast.13, bf16[1024,128]{1,0:T(8,128)(2,1)} %bitcast.14, ...), custom_call_target="tpu_custom_call" | custom-call | tf_op jit(solution)/shard_map/swa_backward/pallas_call | solution.py:514
  50.0 1.0 %write_out.1 = (bf16[2048,128]{1,0:T(8,128)(2,1)}, bf16[1024,128]{1,0:T(8,128)(2,1)}, bf16[1024,128]{1,0:T(8,128)(2,1)}, f32[1,128]{1,0:T(1,128)}, f32[1,128]{1,0:T(1,128)}) custom-call(bf16[2048,128]{1,0:T(8,128)(2,1)S(1)} %get-tuple-element.15.refs_0_, bf16[1024,128]{1,0:T(8,128)(2,1)S(1)} %get-tuple-element.16.refs_1_, ...), custom_call_target="tpu_custom_call" | custom-call | tf_op jit(solution)/shard_map/write_out/pallas_call | solution.py:530

commit v4 on v3

--- a/solution.py
+++ b/solution.py
@@ -45,14 +45,14 @@
     gq_out, gk_out, gv_out, gq_gain_out, gk_gain_out,
     q_buf, g_buf, k_buf, v_buf,
     q_unit, q_inv, k_unit, k_inv, stage,
-    q_ext, q_low, g_t, g_ext,
+    q_ext, q_low, q_unit_t, g_t, g_ext,
     k_raw, kv, v_t, k_t, e_s, ds_s, av_s, dq_t,
     dk_s, dv_s, dq_s,
     send_b, recv_b, send_r, recv_r,
-    red_src, red_y, red_z, red_x,
+    red_src, red_y, red_zx,
     in_sem, up_sem, down_sem,
     f_send, f_recv, s_send, s_recv, b_send, b_recv, r_send, r_recv,
-    ys_sem, yr_sem, zs_sem, zr_sem, xs_sem, xr_sem,
+    ys_sem, yr_sem, zs_sem, zr_sem,
 ):
     n_seq, n_head = sizes
     n_z = n_seq // (CORES * Y_LO)
@@ -86,8 +86,9 @@
         yh = lax.div(r, CORES * Y_LO)
         return ((z * Y_LO + yl) * CORES + c, yh * n_x + x)
 
-    def z_peer(d):
-        return ((lax.rem(z + d, n_z) * Y_LO + y_lo) * CORES + core, head)
+    def zx_peer(d):
+        r = lax.rem(z * n_x + x + d, n_z * n_x)
+        return ((lax.div(r, n_x) * Y_LO + y_lo) * CORES + core, y_hi * n_x + lax.rem(r, n_x))
 
     def x_peer(d):
         return (seq, y_hi * n_x + lax.rem(x + d, n_x))
@@ -221,17 +222,17 @@
         for qb in range(2):
             for h in range(2):
                 rows = rows_of(kh, qb, h)
-                low = (q_unit[rows, :] * qg).astype(BF)
+                unit = q_unit[rows, :]
+                low = (unit * qg).astype(BF)
                 scaled = low.astype(F32) * EXP2_SCALE
                 high = scaled.astype(BF)
                 rest = (scaled - high.astype(F32)).astype(BF)
                 at = slice(h * B, (h + 1) * B)
                 q_low[kh, qb, at, :] = low
+                q_unit_t[kh, qb, :, at] = jnp.transpose(unit)
                 q_ext[kh, qb, at, :D] = high
                 q_ext[kh, qb, at, D:] = rest
                 g_t[kh, qb, :, at] = jnp.transpose(stage[rows, :]).astype(BF)
-    pass_up()
-    pass_down(n_z - 3, n_z)
 
     def prepare_k(sh):
         if sh < 2:
@@ -285,7 +286,7 @@
         g_ext[kh, qb, D : D + EXT, :] = tail.astype(BF)
         g_ext[kh, qb, D + EXT :, :] = jnp.zeros((D - EXT, 2 * B), BF)
 
-    def grads(kh, qb, r0, r1, first_q, first_of):
+    def score_grads(kh, qb, r0, r1):
         off = qb * B
         for b in range(r0, r1, B):
             sh = b // T
@@ -293,21 +294,24 @@
             vx = jnp.concatenate([kv[sh, kh, 1, b % T : b % T + B, :], ones], axis=1)
             dp = dot_nn(vx, g_ext[kh, qb])
             e = e_s[kh, qb, b - off : b - off + B, :]
-            ds = e * dp.astype(BF)
-            ds_s[b - off : b - off + B, :] = ds
-            dv = dot_nt(e, g_ext[kh, qb, :D, :])
-            dk = dot_nn(ds, q_low[kh, qb])
+            ds_s[qb, b - off : b - off + B, :] = e * dp.astype(BF)
+
+    def query_grads(kh, qb):
+        off = qb * B
+        dq_t[kh, qb] = dot_nn(k_t[kh, :, off : off + WINDOW + B], ds_s[qb])
+
+    def key_grads(kh, qb, r0, r1, first_of):
+        off = qb * B
+        for b in range(r0, r1, B):
+            at = slice(b - off, b - off + B)
+            dv = dot_nt(e_s[kh, qb, at, :], g_ext[kh, qb, :D, :])
+            dk = dot_nn(ds_s[qb, at, :], q_low[kh, qb])
             if first_of(b):
                 dv_s[kh, b : b + B, :] = dv
                 dk_s[kh, b : b + B, :] = dk
             else:
                 dv_s[kh, b : b + B, :] += dv
                 dk_s[kh, b : b + B, :] += dk
-        dq = dot_nn(k_t[kh, :, r0:r1], ds_s[r0 - off : r1 - off, :])
-        if first_q:
-            dq_t[kh, qb] = dq
-        else:
-            dq_t[kh, qb] += dq
 
     prepare_k(2)
     for kh in range(2):
@@ -344,6 +348,8 @@
         def _():
             ret_r[kh].start()
 
+    pass_up()
+    pass_down(n_z - 3, n_z)
     take(0)
     prepare_k(0)
     take_b(0)
@@ -352,8 +358,23 @@
         weigh(kh, 0, 0, 2 * T)
         weigh(kh, 1, B, 2 * T)
 
-    q_sum = jnp.zeros((8, D), F32)
-    k_sum = jnp.zeros((8, D), F32)
+    def remote_key_grads(kh):
+        key_grads(kh, 0, 0, 2 * T, lambda b: True)
+        key_grads(kh, 1, B, 2 * T, lambda b: b >= 2 * T)
+        send_b[kh, 0] = (dk_s[kh, T : 2 * T, :] * SCALE).astype(BF)
+        send_b[kh, 1] = dv_s[kh, T : 2 * T, :].astype(BF)
+        ret_b[kh].start()
+
+    def own_key_grads(kh):
+        key_grads(kh, 0, 2 * T, 2 * T + B, lambda b: True)
+        key_grads(kh, 1, 2 * T, 3 * T, lambda b: b >= 2 * T + B)
+
+    def lay_out_queries(kh):
+        for qb in range(2):
+            for h in range(2):
+                dq_s[rows_of(kh, qb, h), :] = jnp.transpose(dq_t[kh, qb, :, h * B : (h + 1) * B]) * SCALE
+
+    gain_sum = jnp.zeros((D, D), F32)
     for kh in range(2):
         if kh == 0:
             take(1)
@@ -364,32 +385,22 @@
         attend(kh, 1, B, 2 * T, False)
         finish(kh, 0)
         finish(kh, 1)
-        grads(kh, 0, 0, 2 * T, True, lambda b: True)
-        grads(kh, 1, B, 2 * T, True, lambda b: False)
-        send_b[kh, 0] = (dk_s[kh, T : 2 * T, :] * SCALE).astype(BF)
-        send_b[kh, 1] = dv_s[kh, T : 2 * T, :].astype(BF)
-        ret_b[kh].start()
+        for qb in range(2):
+            score_grads(kh, qb, qb * B, qb * B + WINDOW + B)
+            query_grads(kh, qb)
+            prod = dq_t[kh, qb] * q_unit_t[kh, qb]
+            for c in range(0, 2 * B, D):
+                gain_sum = gain_sum + prod[:, c : c + D]
         if kh == 0:
+            remote_key_grads(0)
             take(2)
-        grads(kh, 0, 2 * T, 2 * T + B, False, lambda b: True)
-        grads(kh, 1, 2 * T, 3 * T, False, lambda b: b >= 2 * T + B)
-        for sh in range(3):
-            prod = dk_s[kh, sh * T : (sh + 1) * T, :] * kv[sh, kh, 0].astype(F32)
-            k_sum = k_sum + jnp.sum(prod.reshape(T // 8, 8, D), axis=0)
-        for qb in range(2):
-            for h in range(2):
-                rows = rows_of(kh, qb, h)
-                dq = jnp.transpose(dq_t[kh, qb, :, h * B : (h + 1) * B]) * SCALE
-                dq_s[rows, :] = dq
-                q_sum = q_sum + jnp.sum((dq * q_unit[rows, :]).reshape(B // 8, 8, D), axis=0)
-        if kh == 0:
+            own_key_grads(0)
             pay_back(0)
             pass_down(n_z - 5, n_z - 3)
     pass_down(0, n_z - 5)
 
-    k_row = jnp.sum(k_sum, axis=0, keepdims=True) * (SCALE / kg)
-    q_row = jnp.sum(q_sum, axis=0, keepdims=True)
-    red_src[0] = jnp.concatenate([q_row, k_row], axis=0)
+    q_row = jnp.sum(jnp.transpose(gain_sum), axis=0, keepdims=True) * SCALE
+    red_src[0] = q_row
 
     def exchange(level, dst, ssem, rsem, peer, count):
         copies = [
@@ -415,13 +426,15 @@
             m = jnp.mean(du * u, axis=1, keepdims=True)
             out[r : r + B, :] = (inv[r : r + B, :] * (du - u * m)).astype(BF)
 
-    z_copies = exchange(0, red_z, zs_sem, zr_sem, z_peer, n_z)
+    zx_copies = exchange(0, red_zx, zs_sem, zr_sem, zx_peer, n_z * n_x)
+    remote_key_grads(1)
+    own_key_grads(1)
     pay_back(1)
+    lay_out_queries(0)
+    lay_out_queries(1)
     norm_back(dq_s, q_unit, q_inv, qg, gq_out, 4 * T)
-    absorb(0, red_z, z_copies)
-    x_copies = exchange(1, red_x, xs_sem, xr_sem, x_peer, n_x)
-    absorb(1, red_x, x_copies)
-    y_copies = exchange(2, red_y, ys_sem, yr_sem, y_peer, n_y)
+    absorb(0, red_zx, zx_copies)
+    y_copies = exchange(1, red_y, ys_sem, yr_sem, y_peer, n_y)
 
     for kh in range(2):
 
@@ -440,11 +453,11 @@
         )
     norm_back(dq_s, k_unit, k_inv, kg, gk_out, 2 * T)
     gv_out[...] = stage[: 2 * T, :].astype(BF)
-    absorb(2, red_y, y_copies)
-    gq_gain_out[...] = red_src[3, 0:1, :]
-    gk_gain_out[...] = red_src[3, 1:2, :]
-
-    for c in y_copies + z_copies + x_copies + ret_b:
+    absorb(1, red_y, y_copies)
+    gq_gain_out[...] = red_src[2]
+    gk_gain_out[...] = red_src[2] * qg / kg
+
+    for c in y_copies + zx_copies + ret_b:
         c.wait_send()
 
     @pl.when(has_ahead)
@@ -487,28 +500,27 @@
         pltpu.VMEM((2 * T, D), F32), pltpu.VMEM((2 * T, D), F32),
         pltpu.VMEM((4 * T, D), F32),
         pltpu.VMEM((2, 2, 2 * B, 2 * D), BF), pltpu.VMEM((2, 2, 2 * B, D), BF),
+        pltpu.VMEM((2, 2, D, 2 * B), F32),
         pltpu.VMEM((2, 2, D, 2 * B), BF), pltpu.VMEM((2, 2, 2 * D, 2 * B), BF),
         pltpu.VMEM((2, 2 * T, D), BF),
         pltpu.VMEM((3, 2, 2, T, D), BF),
         pltpu.VMEM((2, D + EXT, KEYS), BF),
         pltpu.VMEM((2, D, KEYS), BF),
         pltpu.VMEM((2, 2, WINDOW + B, 2 * B), BF),
-        pltpu.VMEM((WINDOW + B, 2 * B), BF),
+        pltpu.VMEM((2, WINDOW + B, 2 * B), BF),
         pltpu.VMEM((2, 2, D + EXT, 2 * B), F32),
         pltpu.VMEM((2, 2, D, 2 * B), F32),
         pltpu.VMEM((2, KEYS, D), F32), pltpu.VMEM((2, KEYS, D), F32),
         pltpu.VMEM((4 * T, D), F32),
         pltpu.VMEM((2, 2, T, D), BF), pltpu.VMEM((2, 2, T, D), BF),
         pltpu.VMEM((2, 2, T, D), BF), pltpu.VMEM((2, 2, T, D), BF),
-        pltpu.VMEM((4, 2, D), F32),
-        pltpu.VMEM((n_y - 1, 2, D), F32),
-        pltpu.VMEM((max(n_z - 1, 1), 2, D), F32),
-        pltpu.VMEM((max(n_x - 1, 1), 2, D), F32),
+        pltpu.VMEM((3, 1, D), F32),
+        pltpu.VMEM((n_y - 1, 1, D), F32),
+        pltpu.VMEM((n_z * n_x - 1, 1, D), F32),
         dma((4,)), pltpu.SemaphoreType.REGULAR, pltpu.SemaphoreType.REGULAR,
         dma((3,)), dma((3,)), dma((3,)), dma((3,)), dma((2,)), dma((2,)), dma((2,)), dma((2,)),
         dma((n_y - 1,)), dma((n_y - 1,)),
-        dma((max(n_z - 1, 1),)), dma((max(n_z - 1, 1),)),
-        dma((max(n_x - 1, 1),)), dma((max(n_x - 1, 1),)),
+        dma((n_z * n_x - 1,)), dma((n_z * n_x - 1,)),
     ]
     shapes = [((4 * T, D), BF), ((2 * T, D), BF), ((2 * T, D), BF), ((1, D), F32), ((1, D), F32)]
     held = pl.pallas_call(

time: 51.2 us -> 47.9 us (0.936)
  Pallas kernels: 50.4 us -> 47 us
    pallas_call x1, Pallas kernels: 49.4 us -> 46 us  [per_device(): pl.pallas_call(functools.partial(kernel, (n_seq, n_head)), out_shape=[plt...]
where the time goes in v4:
time: 47.9 us; the launch traced here: 47.8 us
  Pallas kernels  47 us (98%)
  between operations  0.8 us (2%)
    pallas_call x1, Pallas kernels, per_device(): pl.pallas_call(functools.partial(kernel, (n_seq, n_head)), out_shape=[plt...  46 us
    pallas_call x1, Pallas kernels, per_device(): pl.pallas_call(write_out, out_shape=[jax.ShapeDtypeStruct(*s) for s in sh...  1.01 us

profile of v4, /device:TPU:1, one launch (start us, length us, event | category | flops | bytes accessed | tf_op | source)
XLA Modules:
  0.0 47.8 jit_solution(7978101430310901293)
XLA Ops:
  0.6 46.0 %swa_backward.1 = (bf16[2048,128]{1,0:T(8,128)(2,1)S(1)}, bf16[1024,128]{1,0:T(8,128)(2,1)S(1)}, bf16[1024,128]{1,0:T(8,128)(2,1)S(1)}, f32[1,128]{1,0:T(1,128)S(1)}, f32[1,128]{1,0:T(1,128)S(1)}) custom-call(bf16[2048,128]{1,0:T(8,128)(2,1)} %bitcast.11, bf16[1024,128]{1,0:T(8,128)(2,1)} %bitcast.13, bf16[1024,128]{1,0:T(8,128)(2,1)} %bitcast.14, ...), custom_call_target="tpu_custom_call" | custom-call | tf_op jit(solution)/shard_map/swa_backward/pallas_call | solution.py:526
  46.6 1.0 %write_out.1 = (bf16[2048,128]{1,0:T(8,128)(2,1)}, bf16[1024,128]{1,0:T(8,128)(2,1)}, bf16[1024,128]{1,0:T(8,128)(2,1)}, f32[1,128]{1,0:T(1,128)}, f32[1,128]{1,0:T(1,128)}) custom-call(bf16[2048,128]{1,0:T(8,128)(2,1)S(1)} %get-tuple-element.15.refs_0_, bf16[1024,128]{1,0:T(8,128)(2,1)S(1)} %get-tuple-element.16.refs_1_, ...), custom_call_target="tpu_custom_call" | custom-call | tf_op jit(solution)/shard_map/write_out/pallas_call | solution.py:542

commit v5 on v4

--- a/solution.py
+++ b/solution.py
@@ -41,7 +41,7 @@
 
 def kernel(
     sizes,
-    q_in, k_in, v_in, g_in, q_gain, k_gain,
+    q_in, k_in, v_in, g_in, q_gain_in, k_gain_in,
     gq_out, gk_out, gv_out, gq_gain_out, gk_gain_out,
     q_buf, g_buf, k_buf, v_buf,
     q_unit, q_inv, k_unit, k_inv, stage,
@@ -50,7 +50,7 @@
     dk_s, dv_s, dq_s,
     send_b, recv_b, send_r, recv_r,
     red_src, red_y, red_zx,
-    in_sem, up_sem, down_sem,
+    gains, in_sem, up_sem, down_sem,
     f_send, f_recv, s_send, s_recv, b_send, b_recv, r_send, r_recv,
     ys_sem, yr_sem, zs_sem, zr_sem,
 ):
@@ -104,7 +104,10 @@
     ins = [
         pltpu.make_async_copy(src, dst, in_sem.at[i])
         for i, (src, dst) in enumerate(
-            ((k_in, k_buf), (v_in, v_buf), (q_in, q_buf), (g_in, g_buf))
+            (
+                (k_in, k_buf), (v_in, v_buf), (q_in, q_buf), (g_in, g_buf),
+                (q_gain_in, gains.at[0]), (k_gain_in, gains.at[1]),
+            )
         )
     ]
     for c in ins:
@@ -146,8 +149,6 @@
             unit[r : r + B, :] = f * i
             inv[r : r + B, :] = jnp.broadcast_to(i, (B, D))
 
-    kg = k_gain[...]
-    qg = q_gain[...]
     def pieces(sh, own):
         return [k_in if own else k_raw.at[sh]] + [kv.at[2 if own else sh, kh, 1] for kh in range(2)]
 
@@ -210,6 +211,10 @@
     def rows_of(kh, qb, h):
         return pl.ds(4 * B * qb + 2 * kh + h, B, stride=4)
 
+    ins[4].wait()
+    ins[5].wait()
+    qg = gains[0]
+    kg = gains[1]
     ins[0].wait()
     normalise(k_buf, k_unit, k_inv, 2 * T)
     for kh in range(2):
@@ -294,18 +299,18 @@
             vx = jnp.concatenate([kv[sh, kh, 1, b % T : b % T + B, :], ones], axis=1)
             dp = dot_nn(vx, g_ext[kh, qb])
             e = e_s[kh, qb, b - off : b - off + B, :]
-            ds_s[qb, b - off : b - off + B, :] = e * dp.astype(BF)
+            ds_s[kh, qb, b - off : b - off + B, :] = e * dp.astype(BF)
 
     def query_grads(kh, qb):
         off = qb * B
-        dq_t[kh, qb] = dot_nn(k_t[kh, :, off : off + WINDOW + B], ds_s[qb])
+        dq_t[kh, qb] = dot_nn(k_t[kh, :, off : off + WINDOW + B], ds_s[kh, qb])
 
     def key_grads(kh, qb, r0, r1, first_of):
         off = qb * B
         for b in range(r0, r1, B):
             at = slice(b - off, b - off + B)
             dv = dot_nt(e_s[kh, qb, at, :], g_ext[kh, qb, :D, :])
-            dk = dot_nn(ds_s[qb, at, :], q_low[kh, qb])
+            dk = dot_nn(ds_s[kh, qb, at, :], q_low[kh, qb])
             if first_of(b):
                 dv_s[kh, b : b + B, :] = dv
                 dk_s[kh, b : b + B, :] = dk
@@ -394,10 +399,9 @@
         if kh == 0:
             remote_key_grads(0)
             take(2)
-            own_key_grads(0)
             pay_back(0)
-            pass_down(n_z - 5, n_z - 3)
-    pass_down(0, n_z - 5)
+            pass_down(n_z - 4, n_z - 3)
+    pass_down(0, n_z - 4)
 
     q_row = jnp.sum(jnp.transpose(gain_sum), axis=0, keepdims=True) * SCALE
     red_src[0] = q_row
@@ -428,8 +432,9 @@
 
     zx_copies = exchange(0, red_zx, zs_sem, zr_sem, zx_peer, n_z * n_x)
     remote_key_grads(1)
+    own_key_grads(0)
+    pay_back(1)
     own_key_grads(1)
-    pay_back(1)
     lay_out_queries(0)
     lay_out_queries(1)
     norm_back(dq_s, q_unit, q_inv, qg, gq_out, 4 * T)
@@ -507,7 +512,7 @@
         pltpu.VMEM((2, D + EXT, KEYS), BF),
         pltpu.VMEM((2, D, KEYS), BF),
         pltpu.VMEM((2, 2, WINDOW + B, 2 * B), BF),
-        pltpu.VMEM((2, WINDOW + B, 2 * B), BF),
+        pltpu.VMEM((2, 2, WINDOW + B, 2 * B), BF),
         pltpu.VMEM((2, 2, D + EXT, 2 * B), F32),
         pltpu.VMEM((2, 2, D, 2 * B), F32),
         pltpu.VMEM((2, KEYS, D), F32), pltpu.VMEM((2, KEYS, D), F32),
@@ -517,7 +522,8 @@
         pltpu.VMEM((3, 1, D), F32),
         pltpu.VMEM((n_y - 1, 1, D), F32),
         pltpu.VMEM((n_z * n_x - 1, 1, D), F32),
-        dma((4,)), pltpu.SemaphoreType.REGULAR, pltpu.SemaphoreType.REGULAR,
+        pltpu.VMEM((2, 1, D), F32),
+        dma((6,)), pltpu.SemaphoreType.REGULAR, pltpu.SemaphoreType.REGULAR,
         dma((3,)), dma((3,)), dma((3,)), dma((3,)), dma((2,)), dma((2,)), dma((2,)), dma((2,)),
         dma((n_y - 1,)), dma((n_y - 1,)),
         dma((n_z * n_x - 1,)), dma((n_z * n_x - 1,)),
@@ -526,7 +532,7 @@
     held = pl.pallas_call(
         functools.partial(kernel, (n_seq, n_head)),
         out_shape=[pltpu.VMEM(*s) for s in shapes],
-        in_specs=[hbm] * 4 + [vmem] * 2,
+        in_specs=[hbm] * 6,
         out_specs=[vmem] * len(shapes),
         scratch_shapes=scratch,
         compiler_params=pltpu.CompilerParams(collective_id=0, has_side_effects=True),

time: 47.9 us -> 47.5 us (level); the launches traced: 47.8 us -> 46.6 us
  Pallas kernels: 47 us -> 46 us
    pallas_call x1, Pallas kernels: 46 us -> 45 us  [per_device(): pl.pallas_call(functools.partial(kernel, (n_seq, n_head)), out_shape=[plt...]
where the time goes in v5:
time: 47.5 us; the launch traced here: 46.6 us
  Pallas kernels  46 us (97%)
  between operations  0.64 us (1%)
    pallas_call x1, Pallas kernels, per_device(): pl.pallas_call(functools.partial(kernel, (n_seq, n_head)), out_shape=[plt...  45 us
    pallas_call x1, Pallas kernels, per_device(): pl.pallas_call(write_out, out_shape=[jax.ShapeDtypeStruct(*s) for s in sh...  1.01 us

profile of v5, /device:TPU:1, one launch (start us, length us, event | category | flops | bytes accessed | tf_op | source)
XLA Modules:
  0.0 46.6 jit_solution(12506652112299793502)
XLA Ops:
  0.6 45.0 %swa_backward.1 = (bf16[2048,128]{1,0:T(8,128)(2,1)S(1)}, bf16[1024,128]{1,0:T(8,128)(2,1)S(1)}, bf16[1024,128]{1,0:T(8,128)(2,1)S(1)}, f32[1,128]{1,0:T(1,128)S(1)}, f32[1,128]{1,0:T(1,128)S(1)}) custom-call(bf16[2048,128]{1,0:T(8,128)(2,1)} %bitcast.11, bf16[1024,128]{1,0:T(8,128)(2,1)} %bitcast.13, bf16[1024,128]{1,0:T(8,128)(2,1)} %bitcast.14, ...), custom_call_target="tpu_custom_call" | custom-call | tf_op jit(solution)/shard_map/swa_backward/pallas_call | solution.py:532
  45.6 1.0 %write_out.1 = (bf16[2048,128]{1,0:T(8,128)(2,1)}, bf16[1024,128]{1,0:T(8,128)(2,1)}, bf16[1024,128]{1,0:T(8,128)(2,1)}, f32[1,128]{1,0:T(1,128)}, f32[1,128]{1,0:T(1,128)}) custom-call(bf16[2048,128]{1,0:T(8,128)(2,1)S(1)} %get-tuple-element.15.refs_0_, bf16[1024,128]{1,0:T(8,128)(2,1)S(1)} %get-tuple-element.16.refs_1_, ...), custom_call_target="tpu_custom_call" | custom-call | tf_op jit(solution)/shard_map/write_out/pallas_call | solution.py:548
